TPU v7x, 512 devices: a whole 4x8x8 slice. The times are simulated.
512 devices in a mesh: row: 8 (over x, core), col: 64 (over z, y).
Axes of the slice: x: 4, y: 8, z: 8, core: 2. Of those that a mesh axis runs over, the one named last changes fastest.
Arguments:
- density: float32 [32768, 1216], P(('row', 'col')), as said below
- pattern: int32 [512, 19], P(('row', 'col')), may hold values from 0 to 1, as said below
Outputs:
- purified: float32 [32768, 1216], P(('row', 'col'))
Inputs may be any that keep to these rules, and one draw needn't show every extreme that they name: pattern[i, s] equals pattern[i + s - 9, 18 - s]; pattern[i, 9] is 1; pattern[i, s] is 0 where i + s - 9 lies outside 0 to 511. `density`: block (i, s) is zero where pattern is 0.
All inputs are finite; a program needn't handle non-finite values.
Results may differ from a plain program's by a relative error of at most 0.007.
Values may be sent and summed in bfloat16 or wider, within the bound.
A program may use at most 64 MiB of HBM per device.

v0:
```python
import jax
import jax.numpy as jnp
from jax import lax
from jax.sharding import PartitionSpec as P

STEPS = 2


def from_behind(value, axis, steps):
    count = lax.axis_size(axis)
    first, last = (max(0, -steps), min(count, count - steps))
    return lax.ppermute(value, axis, [(source, source + steps) for source in range(first, last)])


def apply_mask(values, pattern_rows, block_size):
    rows_total, full_width = values.shape
    blocks = rows_total // block_size
    slot_count = pattern_rows.shape[1]
    shaped = values.reshape(blocks, block_size, slot_count, block_size)
    factor = pattern_rows.astype(jnp.float32)[:, None, :, None]
    return (shaped * factor).reshape(rows_total, full_width)


def band_product(left_rows, far_rows, half_band, block_size):
    rows_total = left_rows.shape[0]
    blocks = rows_total // block_size
    slot_count = 2 * half_band + 1
    outputs = []
    for out_slot in range(slot_count):
        first_slot = max(0, out_slot - half_band)
        last_slot = min(2 * half_band, out_slot + half_band)
        slot_span = last_slot - first_slot + 1
        shift_start = first_slot - out_slot + half_band
        left_part = left_rows[:, first_slot * block_size : (last_slot + 1) * block_size].reshape(
            blocks, block_size, slot_span * block_size
        )
        right_part = far_rows[
            out_slot * block_size : out_slot * block_size + rows_total,
            shift_start * block_size : (shift_start + slot_span) * block_size,
        ].reshape(blocks, block_size, slot_span * block_size)
        outputs.append(
            jnp.einsum("iax,ibx->iab", left_part, right_part, preferred_element_type=jnp.float32)
        )
    return jnp.stack(outputs, axis=2).reshape(rows_total, slot_count * block_size)


def local(density, pattern):
    rows_local, full_width = density.shape
    blocks_local, slot_count = pattern.shape
    block_size = rows_local // blocks_local
    half_band = (slot_count - 1) // 2
    reach_count = (half_band + blocks_local - 1) // blocks_local
    halo_rows = half_band * block_size
    current = density
    for iteration in range(STEPS):
        lowered = current.astype(jnp.bfloat16)
        lower_list = [
            from_behind(lowered, ("row", "col"), distance) for distance in range(reach_count, 0, -1)
        ]
        upper_list = [
            from_behind(lowered, ("row", "col"), -distance)
            for distance in range(1, reach_count + 1)
        ]
        lower_part = jnp.concatenate(lower_list, axis=0)
        upper_part = jnp.concatenate(upper_list, axis=0)
        far_rows = jnp.concatenate([lower_part, lowered, upper_part], axis=0)
        square = apply_mask(
            band_product(lowered, far_rows, half_band, block_size), pattern, block_size
        )
        square_low = square.astype(jnp.bfloat16)
        cube_term = band_product(square_low, far_rows, half_band, block_size)
        current = apply_mask(3.0 * square - 2.0 * cube_term, pattern, block_size)
    return current


def solution(mesh):
    placed = (P(("row", "col"), None), P(("row", "col"), None))
    return jax.shard_map(
        local, mesh=mesh, in_specs=placed, out_specs=P(("row", "col"), None), check_vma=False
    )
```

profile of v0, /device:TPU:61, one launch (start us, length us, event | category | flops | bytes accessed | tf_op | source)
XLA Modules:
  0.0 226.6 jit_solution(8383287280865984737)
XLA Ops:
  0.0 1.0 convert_element_type.51
  1.0 5.0 %collective-permute-start = (bf16[64,1216]{1,0:T(8,128)(2,1)S(1)}, bf16[64,1216]{1,0:T(8,128)(2,1)S(1)}, u32[]{:S(2)}, u32[]{:S(2)}) collective-permute-start(bf16[64,1216]{1,0:T(8,128)(2,1)S(1)} %convert_element_type.51), channel_id=1, source_target_pairs={{0,9},{1,10},{2,11},{3,12},{4,13},{5,14},{6,15},{7,16},{8,17},{9,1... | collective-permute-start | bytes 466952 | tf_op jit(solution)/shard_map/ppermute | solution.py:12
  6.0 4.0 %collective-permute-start.1 = (bf16[64,1216]{1,0:T(8,128)(2,1)S(1)}, bf16[64,1216]{1,0:T(8,128)(2,1)S(1)}, u32[]{:S(2)}, u32[]{:S(2)}) collective-permute-start(bf16[64,1216]{1,0:T(8,128)(2,1)S(1)} %convert_element_type.51), channel_id=1, source_target_pairs={{0,8},{1,9},{2,10},{3,11},{4,12},{5,13},{6,14},{7,15},{8,16},{9,17... | collective-permute-start | bytes 466952 | tf_op jit(solution)/shard_map/ppermute | solution.py:12
  10.0 3.9 %collective-permute-start.2 = (bf16[64,1216]{1,0:T(8,128)(2,1)S(1)}, bf16[64,1216]{1,0:T(8,128)(2,1)S(1)}, u32[]{:S(2)}, u32[]{:S(2)}) collective-permute-start(bf16[64,1216]{1,0:T(8,128)(2,1)S(1)} %convert_element_type.51), channel_id=1, source_target_pairs={{0,7},{1,8},{2,9},{3,10},{4,11},{5,12},{6,13},{7,14},{8,15},{9,16}... | collective-permute-start | bytes 466952 | tf_op jit(solution)/shard_map/ppermute | solution.py:12
  13.9 6.8 %collective-permute-start.3 = (bf16[64,1216]{1,0:T(8,128)(2,1)S(1)}, bf16[64,1216]{1,0:T(8,128)(2,1)S(1)}, u32[]{:S(2)}, u32[]{:S(2)}) collective-permute-start(bf16[64,1216]{1,0:T(8,128)(2,1)S(1)} %convert_element_type.51), channel_id=1, source_target_pairs={{0,6},{1,7},{2,8},{3,9},{4,10},{5,11},{6,12},{7,13},{8,14},{9,15},... | collective-permute-start | bytes 466952 | tf_op jit(solution)/shard_map/ppermute | solution.py:12
  20.7 3.9 %collective-permute-start.4 = (bf16[64,1216]{1,0:T(8,128)(2,1)S(1)}, bf16[64,1216]{1,0:T(8,128)(2,1)S(1)}, u32[]{:S(2)}, u32[]{:S(2)}) collective-permute-start(bf16[64,1216]{1,0:T(8,128)(2,1)S(1)} %convert_element_type.51), channel_id=1, source_target_pairs={{0,5},{1,6},{2,7},{3,8},{4,9},{5,10},{6,11},{7,12},{8,13},{9,14},{... | collective-permute-start | bytes 466952 | tf_op jit(solution)/shard_map/ppermute | solution.py:12
  24.8 5.4 %collective-permute-start.5 = (bf16[64,1216]{1,0:T(8,128)(2,1)S(1)}, bf16[64,1216]{1,0:T(8,128)(2,1)S(1)}, u32[]{:S(2)}, u32[]{:S(2)}) collective-permute-start(bf16[64,1216]{1,0:T(8,128)(2,1)S(1)} %convert_element_type.51), channel_id=1, source_target_pairs={{0,4},{1,5},{2,6},{3,7},{4,8},{5,9},{6,10},{7,11},{8,12},{9,13},{1... | collective-permute-start | bytes 466952 | tf_op jit(solution)/shard_map/ppermute | solution.py:12
  30.5 3.8 %collective-permute-start.6 = (bf16[64,1216]{1,0:T(8,128)(2,1)S(1)}, bf16[64,1216]{1,0:T(8,128)(2,1)S(1)}, u32[]{:S(2)}, u32[]{:S(2)}) collective-permute-start(bf16[64,1216]{1,0:T(8,128)(2,1)S(1)} %convert_element_type.51), channel_id=1, source_target_pairs={{0,3},{1,4},{2,5},{3,6},{4,7},{5,8},{6,9},{7,10},{8,11},{9,12},{10... | collective-permute-start | bytes 466952 | tf_op jit(solution)/shard_map/ppermute | solution.py:12
  34.5 5.2 %collective-permute-start.7 = (bf16[64,1216]{1,0:T(8,128)(2,1)S(1)}, bf16[64,1216]{1,0:T(8,128)(2,1)S(1)}, u32[]{:S(2)}, u32[]{:S(2)}) collective-permute-start(bf16[64,1216]{1,0:T(8,128)(2,1)S(1)} %convert_element_type.51), channel_id=1, source_target_pairs={{0,2},{1,3},{2,4},{3,5},{4,6},{5,7},{6,8},{7,9},{8,10},{9,11},{10,... | collective-permute-start | bytes 466952 | tf_op jit(solution)/shard_map/ppermute | solution.py:12
  39.9 4.3 %collective-permute-start.8 = (bf16[64,1216]{1,0:T(8,128)(2,1)S(1)}, bf16[64,1216]{1,0:T(8,128)(2,1)S(1)}, u32[]{:S(2)}, u32[]{:S(2)}) collective-permute-start(bf16[64,1216]{1,0:T(8,128)(2,1)S(1)} %convert_element_type.51), channel_id=1, source_target_pairs={{0,1},{1,2},{2,3},{3,4},{4,5},{5,6},{6,7},{7,8},{8,9},{9,10},{10,1... | collective-permute-start | bytes 466952 | tf_op jit(solution)/shard_map/ppermute | solution.py:12
  44.4 1.9 collective-permute-start.9
  46.3 0.9 constant_dynamic-update-slice_fusion.14
  47.2 1.9 collective-permute-start.10
  49.4 8.2 %collective-permute-start.11 = (bf16[64,1216]{1,0:T(8,128)(2,1)S(1)}, bf16[64,1216]{1,0:T(8,128)(2,1)S(1)}, u32[]{:S(2)}, u32[]{:S(2)}) collective-permute-start(bf16[64,1216]{1,0:T(8,128)(2,1)S(1)} %convert_element_type.51), channel_id=1, source_target_pairs={{3,0},{4,1},{5,2},{6,3},{7,4},{8,5},{9,6},{10,7},{11,8},{12,9},{13... | collective-permute-start | bytes 466952 | tf_op jit(solution)/shard_map/ppermute | solution.py:12
  57.6 0.9 constant_dynamic-update-slice_fusion.12
  58.4 4.8 %collective-permute-start.12 = (bf16[64,1216]{1,0:T(8,128)(2,1)S(1)}, bf16[64,1216]{1,0:T(8,128)(2,1)S(1)}, u32[]{:S(2)}, u32[]{:S(2)}) collective-permute-start(bf16[64,1216]{1,0:T(8,128)(2,1)S(1)} %convert_element_type.51), channel_id=1, source_target_pairs={{4,0},{5,1},{6,2},{7,3},{8,4},{9,5},{10,6},{11,7},{12,8},{13,9},{1... | collective-permute-start | bytes 466952 | tf_op jit(solution)/shard_map/ppermute | solution.py:12
  64.0 6.8 %collective-permute-start.13 = (bf16[64,1216]{1,0:T(8,128)(2,1)S(1)}, bf16[64,1216]{1,0:T(8,128)(2,1)S(1)}, u32[]{:S(2)}, u32[]{:S(2)}) collective-permute-start(bf16[64,1216]{1,0:T(8,128)(2,1)S(1)} %convert_element_type.51), channel_id=1, source_target_pairs={{5,0},{6,1},{7,2},{8,3},{9,4},{10,5},{11,6},{12,7},{13,8},{14,9},{... | collective-permute-start | bytes 466952 | tf_op jit(solution)/shard_map/ppermute | solution.py:12
  70.9 0.9 constant_dynamic-update-slice_fusion.10
  71.9 4.8 %collective-permute-start.14 = (bf16[64,1216]{1,0:T(8,128)(2,1)S(1)}, bf16[64,1216]{1,0:T(8,128)(2,1)S(1)}, u32[]{:S(2)}, u32[]{:S(2)}) collective-permute-start(bf16[64,1216]{1,0:T(8,128)(2,1)S(1)} %convert_element_type.51), channel_id=1, source_target_pairs={{6,0},{7,1},{8,2},{9,3},{10,4},{11,5},{12,6},{13,7},{14,8},{15,9},... | collective-permute-start | bytes 466952 | tf_op jit(solution)/shard_map/ppermute | solution.py:12
  76.7 0.9 constant_dynamic-update-slice_fusion.8
  77.6 4.1 %collective-permute-start.15 = (bf16[64,1216]{1,0:T(8,128)(2,1)S(1)}, bf16[64,1216]{1,0:T(8,128)(2,1)S(1)}, u32[]{:S(2)}, u32[]{:S(2)}) collective-permute-start(bf16[64,1216]{1,0:T(8,128)(2,1)S(1)} %convert_element_type.51), channel_id=1, source_target_pairs={{7,0},{8,1},{9,2},{10,3},{11,4},{12,5},{13,6},{14,7},{15,8},{16,9}... | collective-permute-start | bytes 466952 | tf_op jit(solution)/shard_map/ppermute | solution.py:12
  82.5 7.9 %collective-permute-start.16 = (bf16[64,1216]{1,0:T(8,128)(2,1)S(1)}, bf16[64,1216]{1,0:T(8,128)(2,1)S(1)}, u32[]{:S(2)}, u32[]{:S(2)}) collective-permute-start(bf16[64,1216]{1,0:T(8,128)(2,1)S(1)} %convert_element_type.51), channel_id=1, source_target_pairs={{8,0},{9,1},{10,2},{11,3},{12,4},{13,5},{14,6},{15,7},{16,8},{17,9... | collective-permute-start | bytes 466952 | tf_op jit(solution)/shard_map/ppermute | solution.py:12
  90.3 0.8 constant_dynamic-update-slice_fusion.6
  91.2 1.9 collective-permute-start.17
  93.3 0.8 constant_dynamic-update-slice_fusion.4
  94.3 1.3 collective-permute-done.15
  96.4 6.3 %collective-permute-done.16 = bf16[64,1216]{1,0:T(8,128)(2,1)S(1)} collective-permute-done((bf16[64,1216]{1,0:T(8,128)(2,1)S(1)}, bf16[64,1216]{1,0:T(8,128)(2,1)S(1)}, u32[]{:S(2)}, u32[]{:S(2)}) %collective-permute-start.16) | collective-permute-done | bytes 155680 | tf_op jit(solution)/shard_map/ppermute | solution.py:12
  113.4 1.9 collective-permute-start.18
  115.4 1.9 collective-permute-start.19
  117.3 3.2 %collective-permute-start.20 = (bf16[64,1216]{1,0:T(8,128)(2,1)S(1)}, bf16[64,1216]{1,0:T(8,128)(2,1)S(1)}, u32[]{:S(2)}, u32[]{:S(2)}) collective-permute-start(bf16[64,1216]{1,0:T(8,128)(2,1)S(1)} %multiply_convert_fusion.2), channel_id=1, source_target_pairs={{0,7},{1,8},{2,9},{3,10},{4,11},{5,12},{6,13},{7,14},{8,15},{9,16}... | collective-permute-start | bytes 466952 | tf_op jit(solution)/shard_map/ppermute | solution.py:12
  120.5 1.9 collective-permute-start.21
  122.4 1.9 collective-permute-start.22
  132.5 6.1 %collective-permute-start.23 = (bf16[64,1216]{1,0:T(8,128)(2,1)S(1)}, bf16[64,1216]{1,0:T(8,128)(2,1)S(1)}, u32[]{:S(2)}, u32[]{:S(2)}) collective-permute-start(bf16[64,1216]{1,0:T(8,128)(2,1)S(1)} %multiply_convert_fusion.2), channel_id=1, source_target_pairs={{0,4},{1,5},{2,6},{3,7},{4,8},{5,9},{6,10},{7,11},{8,12},{9,13},{1... | collective-permute-start | bytes 466952 | tf_op jit(solution)/shard_map/ppermute | solution.py:12
  138.8 1.9 collective-permute-start.24
  141.0 5.4 %collective-permute-start.25 = (bf16[64,1216]{1,0:T(8,128)(2,1)S(1)}, bf16[64,1216]{1,0:T(8,128)(2,1)S(1)}, u32[]{:S(2)}, u32[]{:S(2)}) collective-permute-start(bf16[64,1216]{1,0:T(8,128)(2,1)S(1)} %multiply_convert_fusion.2), channel_id=1, source_target_pairs={{0,2},{1,3},{2,4},{3,5},{4,6},{5,7},{6,8},{7,9},{8,10},{9,11},{10,... | collective-permute-start | bytes 466952 | tf_op jit(solution)/shard_map/ppermute | solution.py:12
  146.6 5.3 %collective-permute-start.26 = (bf16[64,1216]{1,0:T(8,128)(2,1)S(1)}, bf16[64,1216]{1,0:T(8,128)(2,1)S(1)}, u32[]{:S(2)}, u32[]{:S(2)}) collective-permute-start(bf16[64,1216]{1,0:T(8,128)(2,1)S(1)} %multiply_convert_fusion.2), channel_id=1, source_target_pairs={{0,1},{1,2},{2,3},{3,4},{4,5},{5,6},{6,7},{7,8},{8,9},{9,10},{10,1... | collective-permute-start | bytes 466952 | tf_op jit(solution)/shard_map/ppermute | solution.py:12
  152.2 1.9 collective-permute-start.27
  154.4 1.9 collective-permute-start.28
  156.5 5.0 %collective-permute-start.29 = (bf16[64,1216]{1,0:T(8,128)(2,1)S(1)}, bf16[64,1216]{1,0:T(8,128)(2,1)S(1)}, u32[]{:S(2)}, u32[]{:S(2)}) collective-permute-start(bf16[64,1216]{1,0:T(8,128)(2,1)S(1)} %multiply_convert_fusion.2), channel_id=1, source_target_pairs={{3,0},{4,1},{5,2},{6,3},{7,4},{8,5},{9,6},{10,7},{11,8},{12,9},{13... | collective-permute-start | bytes 466952 | tf_op jit(solution)/shard_map/ppermute | solution.py:12
  161.8 1.4 collective-permute-done.25
  163.2 5.8 %collective-permute-start.30 = (bf16[64,1216]{1,0:T(8,128)(2,1)S(1)}, bf16[64,1216]{1,0:T(8,128)(2,1)S(1)}, u32[]{:S(2)}, u32[]{:S(2)}) collective-permute-start(bf16[64,1216]{1,0:T(8,128)(2,1)S(1)} %multiply_convert_fusion.2), channel_id=1, source_target_pairs={{4,0},{5,1},{6,2},{7,3},{8,4},{9,5},{10,6},{11,7},{12,8},{13,9},{1... | collective-permute-start | bytes 466952 | tf_op jit(solution)/shard_map/ppermute | solution.py:12
  169.2 9.2 %collective-permute-start.31 = (bf16[64,1216]{1,0:T(8,128)(2,1)S(1)}, bf16[64,1216]{1,0:T(8,128)(2,1)S(1)}, u32[]{:S(2)}, u32[]{:S(2)}) collective-permute-start(bf16[64,1216]{1,0:T(8,128)(2,1)S(1)} %multiply_convert_fusion.2), channel_id=1, source_target_pairs={{5,0},{6,1},{7,2},{8,3},{9,4},{10,5},{11,6},{12,7},{13,8},{14,9},{... | collective-permute-start | bytes 466952 | tf_op jit(solution)/shard_map/ppermute | solution.py:12
  178.9 4.1 %collective-permute-start.32 = (bf16[64,1216]{1,0:T(8,128)(2,1)S(1)}, bf16[64,1216]{1,0:T(8,128)(2,1)S(1)}, u32[]{:S(2)}, u32[]{:S(2)}) collective-permute-start(bf16[64,1216]{1,0:T(8,128)(2,1)S(1)} %multiply_convert_fusion.2), channel_id=1, source_target_pairs={{6,0},{7,1},{8,2},{9,3},{10,4},{11,5},{12,6},{13,7},{14,8},{15,9},... | collective-permute-start | bytes 466952 | tf_op jit(solution)/shard_map/ppermute | solution.py:12
  183.2 7.2 %collective-permute-start.33 = (bf16[64,1216]{1,0:T(8,128)(2,1)S(1)}, bf16[64,1216]{1,0:T(8,128)(2,1)S(1)}, u32[]{:S(2)}, u32[]{:S(2)}) collective-permute-start(bf16[64,1216]{1,0:T(8,128)(2,1)S(1)} %multiply_convert_fusion.2), channel_id=1, source_target_pairs={{7,0},{8,1},{9,2},{10,3},{11,4},{12,5},{13,6},{14,7},{15,8},{16,9}... | collective-permute-start | bytes 466952 | tf_op jit(solution)/shard_map/ppermute | solution.py:12
  190.7 2.3 %collective-permute-start.34 = (bf16[64,1216]{1,0:T(8,128)(2,1)S(1)}, bf16[64,1216]{1,0:T(8,128)(2,1)S(1)}, u32[]{:S(2)}, u32[]{:S(2)}) collective-permute-start(bf16[64,1216]{1,0:T(8,128)(2,1)S(1)} %multiply_convert_fusion.2), channel_id=1, source_target_pairs={{8,0},{9,1},{10,2},{11,3},{12,4},{13,5},{14,6},{15,7},{16,8},{17,9... | collective-permute-start | bytes 466952 | tf_op jit(solution)/shard_map/ppermute | solution.py:12
  193.2 5.9 %collective-permute-start.35 = (bf16[64,1216]{1,0:T(8,128)(2,1)S(1)}, bf16[64,1216]{1,0:T(8,128)(2,1)S(1)}, u32[]{:S(2)}, u32[]{:S(2)}) collective-permute-start(bf16[64,1216]{1,0:T(8,128)(2,1)S(1)} %multiply_convert_fusion.2), channel_id=1, source_target_pairs={{9,0},{10,1},{11,2},{12,3},{13,4},{14,5},{15,6},{16,7},{17,8},{18,... | collective-permute-start | bytes 466952 | tf_op jit(solution)/shard_map/ppermute | solution.py:12
  200.0 1.3 collective-permute-done.33
  201.5 8.6 %collective-permute-done.34 = bf16[64,1216]{1,0:T(8,128)(2,1)S(1)} collective-permute-done((bf16[64,1216]{1,0:T(8,128)(2,1)S(1)}, bf16[64,1216]{1,0:T(8,128)(2,1)S(1)}, u32[]{:S(2)}, u32[]{:S(2)}) %collective-permute-start.34) | collective-permute-done | bytes 155680 | tf_op jit(solution)/shard_map/ppermute | solution.py:12
  (273 shorter events, 42.5 us)
Async XLA Ops:
  0.0 24.6 %copy-start.48 = (s32[1,19]{1,0:T(1,128)S(1)}, s32[1,19]{1,0:T(1,128)}, u32[]{:S(2)}) copy-start(s32[1,19]{1,0:T(1,128)} %param.3) | copy-start | bytes 232
  1.0 23.8 %collective-permute-start = (bf16[64,1216]{1,0:T(8,128)(2,1)S(1)}, bf16[64,1216]{1,0:T(8,128)(2,1)S(1)}, u32[]{:S(2)}, u32[]{:S(2)}) collective-permute-start(bf16[64,1216]{1,0:T(8,128)(2,1)S(1)} %convert_element_type.51), channel_id=1, source_target_pairs={{0,9},{1,10},{2,11},{3,12},{4,13},{5,14},{6,15},{7,16},{8,17},{9,1... | collective-permute-start | bytes 466952 | tf_op jit(solution)/shard_map/ppermute | solution.py:12
  6.0 24.4 %collective-permute-start.1 = (bf16[64,1216]{1,0:T(8,128)(2,1)S(1)}, bf16[64,1216]{1,0:T(8,128)(2,1)S(1)}, u32[]{:S(2)}, u32[]{:S(2)}) collective-permute-start(bf16[64,1216]{1,0:T(8,128)(2,1)S(1)} %convert_element_type.51), channel_id=1, source_target_pairs={{0,8},{1,9},{2,10},{3,11},{4,12},{5,13},{6,14},{7,15},{8,16},{9,17... | collective-permute-start | bytes 466952 | tf_op jit(solution)/shard_map/ppermute | solution.py:12
  10.0 24.4 %collective-permute-start.2 = (bf16[64,1216]{1,0:T(8,128)(2,1)S(1)}, bf16[64,1216]{1,0:T(8,128)(2,1)S(1)}, u32[]{:S(2)}, u32[]{:S(2)}) collective-permute-start(bf16[64,1216]{1,0:T(8,128)(2,1)S(1)} %convert_element_type.51), channel_id=1, source_target_pairs={{0,7},{1,8},{2,9},{3,10},{4,11},{5,12},{6,13},{7,14},{8,15},{9,16}... | collective-permute-start | bytes 466952 | tf_op jit(solution)/shard_map/ppermute | solution.py:12
  13.9 26.0 %collective-permute-start.3 = (bf16[64,1216]{1,0:T(8,128)(2,1)S(1)}, bf16[64,1216]{1,0:T(8,128)(2,1)S(1)}, u32[]{:S(2)}, u32[]{:S(2)}) collective-permute-start(bf16[64,1216]{1,0:T(8,128)(2,1)S(1)} %convert_element_type.51), channel_id=1, source_target_pairs={{0,6},{1,7},{2,8},{3,9},{4,10},{5,11},{6,12},{7,13},{8,14},{9,15},... | collective-permute-start | bytes 466952 | tf_op jit(solution)/shard_map/ppermute | solution.py:12
  20.7 23.7 %collective-permute-start.4 = (bf16[64,1216]{1,0:T(8,128)(2,1)S(1)}, bf16[64,1216]{1,0:T(8,128)(2,1)S(1)}, u32[]{:S(2)}, u32[]{:S(2)}) collective-permute-start(bf16[64,1216]{1,0:T(8,128)(2,1)S(1)} %convert_element_type.51), channel_id=1, source_target_pairs={{0,5},{1,6},{2,7},{3,8},{4,9},{5,10},{6,11},{7,12},{8,13},{9,14},{... | collective-permute-start | bytes 466952 | tf_op jit(solution)/shard_map/ppermute | solution.py:12
  24.8 22.4 %collective-permute-start.5 = (bf16[64,1216]{1,0:T(8,128)(2,1)S(1)}, bf16[64,1216]{1,0:T(8,128)(2,1)S(1)}, u32[]{:S(2)}, u32[]{:S(2)}) collective-permute-start(bf16[64,1216]{1,0:T(8,128)(2,1)S(1)} %convert_element_type.51), channel_id=1, source_target_pairs={{0,4},{1,5},{2,6},{3,7},{4,8},{5,9},{6,10},{7,11},{8,12},{9,13},{1... | collective-permute-start | bytes 466952 | tf_op jit(solution)/shard_map/ppermute | solution.py:12
  30.5 18.9 %collective-permute-start.6 = (bf16[64,1216]{1,0:T(8,128)(2,1)S(1)}, bf16[64,1216]{1,0:T(8,128)(2,1)S(1)}, u32[]{:S(2)}, u32[]{:S(2)}) collective-permute-start(bf16[64,1216]{1,0:T(8,128)(2,1)S(1)} %convert_element_type.51), channel_id=1, source_target_pairs={{0,3},{1,4},{2,5},{3,6},{4,7},{5,8},{6,9},{7,10},{8,11},{9,12},{10... | collective-permute-start | bytes 466952 | tf_op jit(solution)/shard_map/ppermute | solution.py:12
  34.5 24.0 %collective-permute-start.7 = (bf16[64,1216]{1,0:T(8,128)(2,1)S(1)}, bf16[64,1216]{1,0:T(8,128)(2,1)S(1)}, u32[]{:S(2)}, u32[]{:S(2)}) collective-permute-start(bf16[64,1216]{1,0:T(8,128)(2,1)S(1)} %convert_element_type.51), channel_id=1, source_target_pairs={{0,2},{1,3},{2,4},{3,5},{4,6},{5,7},{6,8},{7,9},{8,10},{9,11},{10,... | collective-permute-start | bytes 466952 | tf_op jit(solution)/shard_map/ppermute | solution.py:12
  39.9 24.1 %collective-permute-start.8 = (bf16[64,1216]{1,0:T(8,128)(2,1)S(1)}, bf16[64,1216]{1,0:T(8,128)(2,1)S(1)}, u32[]{:S(2)}, u32[]{:S(2)}) collective-permute-start(bf16[64,1216]{1,0:T(8,128)(2,1)S(1)} %convert_element_type.51), channel_id=1, source_target_pairs={{0,1},{1,2},{2,3},{3,4},{4,5},{5,6},{6,7},{7,8},{8,9},{9,10},{10,1... | collective-permute-start | bytes 466952 | tf_op jit(solution)/shard_map/ppermute | solution.py:12
  44.4 27.5 %collective-permute-start.9 = (bf16[64,1216]{1,0:T(8,128)(2,1)S(1)}, bf16[64,1216]{1,0:T(8,128)(2,1)S(1)}, u32[]{:S(2)}, u32[]{:S(2)}) collective-permute-start(bf16[64,1216]{1,0:T(8,128)(2,1)S(1)} %convert_element_type.51), channel_id=1, source_target_pairs={{1,0},{2,1},{3,2},{4,3},{5,4},{6,5},{7,6},{8,7},{9,8},{10,9},{11,1... | collective-permute-start | bytes 466952 | tf_op jit(solution)/shard_map/ppermute | solution.py:12
  47.2 30.4 %collective-permute-start.10 = (bf16[64,1216]{1,0:T(8,128)(2,1)S(1)}, bf16[64,1216]{1,0:T(8,128)(2,1)S(1)}, u32[]{:S(2)}, u32[]{:S(2)}) collective-permute-start(bf16[64,1216]{1,0:T(8,128)(2,1)S(1)} %convert_element_type.51), channel_id=1, source_target_pairs={{2,0},{3,1},{4,2},{5,3},{6,4},{7,5},{8,6},{9,7},{10,8},{11,9},{12,... | collective-permute-start | bytes 466952 | tf_op jit(solution)/shard_map/ppermute | solution.py:12
  49.4 9.1 %copy-start.38 = (bf16[64,1216]{1,0:T(8,128)(2,1)}, bf16[64,1216]{1,0:T(8,128)(2,1)S(1)}, u32[]{:S(2)}) copy-start(bf16[64,1216]{1,0:T(8,128)(2,1)S(1)} %collective-permute-done.6) | copy-start | bytes 466948
  49.4 33.1 %collective-permute-start.11 = (bf16[64,1216]{1,0:T(8,128)(2,1)S(1)}, bf16[64,1216]{1,0:T(8,128)(2,1)S(1)}, u32[]{:S(2)}, u32[]{:S(2)}) collective-permute-start(bf16[64,1216]{1,0:T(8,128)(2,1)S(1)} %convert_element_type.51), channel_id=1, source_target_pairs={{3,0},{4,1},{5,2},{6,3},{7,4},{8,5},{9,6},{10,7},{11,8},{12,9},{13... | collective-permute-start | bytes 466952 | tf_op jit(solution)/shard_map/ppermute | solution.py:12
  58.4 32.7 %collective-permute-start.12 = (bf16[64,1216]{1,0:T(8,128)(2,1)S(1)}, bf16[64,1216]{1,0:T(8,128)(2,1)S(1)}, u32[]{:S(2)}, u32[]{:S(2)}) collective-permute-start(bf16[64,1216]{1,0:T(8,128)(2,1)S(1)} %convert_element_type.51), channel_id=1, source_target_pairs={{4,0},{5,1},{6,2},{7,3},{8,4},{9,5},{10,6},{11,7},{12,8},{13,9},{1... | collective-permute-start | bytes 466952 | tf_op jit(solution)/shard_map/ppermute | solution.py:12
  64.0 7.7 %copy-start.40 = (bf16[64,1216]{1,0:T(8,128)(2,1)}, bf16[64,1216]{1,0:T(8,128)(2,1)S(1)}, u32[]{:S(2)}) copy-start(bf16[64,1216]{1,0:T(8,128)(2,1)S(1)} %collective-permute-done.8) | copy-start | bytes 466948
  64.0 29.3 %collective-permute-start.13 = (bf16[64,1216]{1,0:T(8,128)(2,1)S(1)}, bf16[64,1216]{1,0:T(8,128)(2,1)S(1)}, u32[]{:S(2)}, u32[]{:S(2)}) collective-permute-start(bf16[64,1216]{1,0:T(8,128)(2,1)S(1)} %convert_element_type.51), channel_id=1, source_target_pairs={{5,0},{6,1},{7,2},{8,3},{9,4},{10,5},{11,6},{12,7},{13,8},{14,9},{... | collective-permute-start | bytes 466952 | tf_op jit(solution)/shard_map/ppermute | solution.py:12
  71.9 5.7 %copy-start.42 = (bf16[64,1216]{1,0:T(8,128)(2,1)}, bf16[64,1216]{1,0:T(8,128)(2,1)S(1)}, u32[]{:S(2)}) copy-start(bf16[64,1216]{1,0:T(8,128)(2,1)S(1)} %collective-permute-done.9) | copy-start | bytes 466948
  71.9 22.2 %collective-permute-start.14 = (bf16[64,1216]{1,0:T(8,128)(2,1)S(1)}, bf16[64,1216]{1,0:T(8,128)(2,1)S(1)}, u32[]{:S(2)}, u32[]{:S(2)}) collective-permute-start(bf16[64,1216]{1,0:T(8,128)(2,1)S(1)} %convert_element_type.51), channel_id=1, source_target_pairs={{6,0},{7,1},{8,2},{9,3},{10,4},{11,5},{12,6},{13,7},{14,8},{15,9},... | collective-permute-start | bytes 466952 | tf_op jit(solution)/shard_map/ppermute | solution.py:12
  77.6 18.0 %collective-permute-start.15 = (bf16[64,1216]{1,0:T(8,128)(2,1)S(1)}, bf16[64,1216]{1,0:T(8,128)(2,1)S(1)}, u32[]{:S(2)}, u32[]{:S(2)}) collective-permute-start(bf16[64,1216]{1,0:T(8,128)(2,1)S(1)} %convert_element_type.51), channel_id=1, source_target_pairs={{7,0},{8,1},{9,2},{10,3},{11,4},{12,5},{13,6},{14,7},{15,8},{16,9}... | collective-permute-start | bytes 466952 | tf_op jit(solution)/shard_map/ppermute | solution.py:12
  82.5 8.7 %copy-start.44 = (bf16[64,1216]{1,0:T(8,128)(2,1)}, bf16[64,1216]{1,0:T(8,128)(2,1)S(1)}, u32[]{:S(2)}) copy-start(bf16[64,1216]{1,0:T(8,128)(2,1)S(1)} %collective-permute-done.11) | copy-start | bytes 466948
  82.5 20.2 %collective-permute-start.16 = (bf16[64,1216]{1,0:T(8,128)(2,1)S(1)}, bf16[64,1216]{1,0:T(8,128)(2,1)S(1)}, u32[]{:S(2)}, u32[]{:S(2)}) collective-permute-start(bf16[64,1216]{1,0:T(8,128)(2,1)S(1)} %convert_element_type.51), channel_id=1, source_target_pairs={{8,0},{9,1},{10,2},{11,3},{12,4},{13,5},{14,6},{15,7},{16,8},{17,9... | collective-permute-start | bytes 466952 | tf_op jit(solution)/shard_map/ppermute | solution.py:12
  91.2 12.3 %collective-permute-start.17 = (bf16[64,1216]{1,0:T(8,128)(2,1)S(1)}, bf16[64,1216]{1,0:T(8,128)(2,1)S(1)}, u32[]{:S(2)}, u32[]{:S(2)}) collective-permute-start(bf16[64,1216]{1,0:T(8,128)(2,1)S(1)} %convert_element_type.51), channel_id=1, source_target_pairs={{9,0},{10,1},{11,2},{12,3},{13,4},{14,5},{15,6},{16,7},{17,8},{18,... | collective-permute-start | bytes 466952 | tf_op jit(solution)/shard_map/ppermute | solution.py:12
  113.4 19.0 %collective-permute-start.18 = (bf16[64,1216]{1,0:T(8,128)(2,1)S(1)}, bf16[64,1216]{1,0:T(8,128)(2,1)S(1)}, u32[]{:S(2)}, u32[]{:S(2)}) collective-permute-start(bf16[64,1216]{1,0:T(8,128)(2,1)S(1)} %multiply_convert_fusion.2), channel_id=1, source_target_pairs={{0,9},{1,10},{2,11},{3,12},{4,13},{5,14},{6,15},{7,16},{8,17},{9,1... | collective-permute-start | bytes 466952 | tf_op jit(solution)/shard_map/ppermute | solution.py:12
  115.4 23.4 %collective-permute-start.19 = (bf16[64,1216]{1,0:T(8,128)(2,1)S(1)}, bf16[64,1216]{1,0:T(8,128)(2,1)S(1)}, u32[]{:S(2)}, u32[]{:S(2)}) collective-permute-start(bf16[64,1216]{1,0:T(8,128)(2,1)S(1)} %multiply_convert_fusion.2), channel_id=1, source_target_pairs={{0,8},{1,9},{2,10},{3,11},{4,12},{5,13},{6,14},{7,15},{8,16},{9,17... | collective-permute-start | bytes 466952 | tf_op jit(solution)/shard_map/ppermute | solution.py:12
  117.3 23.6 %collective-permute-start.20 = (bf16[64,1216]{1,0:T(8,128)(2,1)S(1)}, bf16[64,1216]{1,0:T(8,128)(2,1)S(1)}, u32[]{:S(2)}, u32[]{:S(2)}) collective-permute-start(bf16[64,1216]{1,0:T(8,128)(2,1)S(1)} %multiply_convert_fusion.2), channel_id=1, source_target_pairs={{0,7},{1,8},{2,9},{3,10},{4,11},{5,12},{6,13},{7,14},{8,15},{9,16}... | collective-permute-start | bytes 466952 | tf_op jit(solution)/shard_map/ppermute | solution.py:12
  120.5 26.1 %collective-permute-start.21 = (bf16[64,1216]{1,0:T(8,128)(2,1)S(1)}, bf16[64,1216]{1,0:T(8,128)(2,1)S(1)}, u32[]{:S(2)}, u32[]{:S(2)}) collective-permute-start(bf16[64,1216]{1,0:T(8,128)(2,1)S(1)} %multiply_convert_fusion.2), channel_id=1, source_target_pairs={{0,6},{1,7},{2,8},{3,9},{4,10},{5,11},{6,12},{7,13},{8,14},{9,15},... | collective-permute-start | bytes 466952 | tf_op jit(solution)/shard_map/ppermute | solution.py:12
  122.4 29.7 %collective-permute-start.22 = (bf16[64,1216]{1,0:T(8,128)(2,1)S(1)}, bf16[64,1216]{1,0:T(8,128)(2,1)S(1)}, u32[]{:S(2)}, u32[]{:S(2)}) collective-permute-start(bf16[64,1216]{1,0:T(8,128)(2,1)S(1)} %multiply_convert_fusion.2), channel_id=1, source_target_pairs={{0,5},{1,6},{2,7},{3,8},{4,9},{5,10},{6,11},{7,12},{8,13},{9,14},{... | collective-permute-start | bytes 466952 | tf_op jit(solution)/shard_map/ppermute | solution.py:12
  132.4 8.3 %copy-start.14 = (bf16[64,1216]{1,0:T(8,128)(2,1)}, bf16[64,1216]{1,0:T(8,128)(2,1)S(1)}, u32[]{:S(2)}) copy-start(bf16[64,1216]{1,0:T(8,128)(2,1)S(1)} %collective-permute-done.18) | copy-start | bytes 466948
  132.5 21.9 %collective-permute-start.23 = (bf16[64,1216]{1,0:T(8,128)(2,1)S(1)}, bf16[64,1216]{1,0:T(8,128)(2,1)S(1)}, u32[]{:S(2)}, u32[]{:S(2)}) collective-permute-start(bf16[64,1216]{1,0:T(8,128)(2,1)S(1)} %multiply_convert_fusion.2), channel_id=1, source_target_pairs={{0,4},{1,5},{2,6},{3,7},{4,8},{5,9},{6,10},{7,11},{8,12},{9,13},{1... | collective-permute-start | bytes 466952 | tf_op jit(solution)/shard_map/ppermute | solution.py:12
  138.8 7.7 %copy-start.6 = (bf16[64,1216]{1,0:T(8,128)(2,1)}, bf16[64,1216]{1,0:T(8,128)(2,1)S(1)}, u32[]{:S(2)}) copy-start(bf16[64,1216]{1,0:T(8,128)(2,1)S(1)} %collective-permute-done.19) | copy-start | bytes 466948
  138.8 17.6 %collective-permute-start.24 = (bf16[64,1216]{1,0:T(8,128)(2,1)S(1)}, bf16[64,1216]{1,0:T(8,128)(2,1)S(1)}, u32[]{:S(2)}, u32[]{:S(2)}) collective-permute-start(bf16[64,1216]{1,0:T(8,128)(2,1)S(1)} %multiply_convert_fusion.2), channel_id=1, source_target_pairs={{0,3},{1,4},{2,5},{3,6},{4,7},{5,8},{6,9},{7,10},{8,11},{9,12},{10... | collective-permute-start | bytes 466952 | tf_op jit(solution)/shard_map/ppermute | solution.py:12
  141.0 11.2 %copy-start.8 = (bf16[64,1216]{1,0:T(8,128)(2,1)}, bf16[64,1216]{1,0:T(8,128)(2,1)S(1)}, u32[]{:S(2)}) copy-start(bf16[64,1216]{1,0:T(8,128)(2,1)S(1)} %collective-permute-done.20) | copy-start | bytes 466948
  141.0 22.2 %collective-permute-start.25 = (bf16[64,1216]{1,0:T(8,128)(2,1)S(1)}, bf16[64,1216]{1,0:T(8,128)(2,1)S(1)}, u32[]{:S(2)}, u32[]{:S(2)}) collective-permute-start(bf16[64,1216]{1,0:T(8,128)(2,1)S(1)} %multiply_convert_fusion.2), channel_id=1, source_target_pairs={{0,2},{1,3},{2,4},{3,5},{4,6},{5,7},{6,8},{7,9},{8,10},{9,11},{10,... | collective-permute-start | bytes 466952 | tf_op jit(solution)/shard_map/ppermute | solution.py:12
  146.6 7.8 %copy-start.4 = (bf16[64,1216]{1,0:T(8,128)(2,1)}, bf16[64,1216]{1,0:T(8,128)(2,1)S(1)}, u32[]{:S(2)}) copy-start(bf16[64,1216]{1,0:T(8,128)(2,1)S(1)} %collective-permute-done.21) | copy-start | bytes 466948
  146.6 22.6 %collective-permute-start.26 = (bf16[64,1216]{1,0:T(8,128)(2,1)S(1)}, bf16[64,1216]{1,0:T(8,128)(2,1)S(1)}, u32[]{:S(2)}, u32[]{:S(2)}) collective-permute-start(bf16[64,1216]{1,0:T(8,128)(2,1)S(1)} %multiply_convert_fusion.2), channel_id=1, source_target_pairs={{0,1},{1,2},{2,3},{3,4},{4,5},{5,6},{6,7},{7,8},{8,9},{9,10},{10,1... | collective-permute-start | bytes 466952 | tf_op jit(solution)/shard_map/ppermute | solution.py:12
  152.2 26.8 %collective-permute-start.27 = (bf16[64,1216]{1,0:T(8,128)(2,1)S(1)}, bf16[64,1216]{1,0:T(8,128)(2,1)S(1)}, u32[]{:S(2)}, u32[]{:S(2)}) collective-permute-start(bf16[64,1216]{1,0:T(8,128)(2,1)S(1)} %multiply_convert_fusion.2), channel_id=1, source_target_pairs={{1,0},{2,1},{3,2},{4,3},{5,4},{6,5},{7,6},{8,7},{9,8},{10,9},{11,1... | collective-permute-start | bytes 466952 | tf_op jit(solution)/shard_map/ppermute | solution.py:12
  154.4 28.9 %collective-permute-start.28 = (bf16[64,1216]{1,0:T(8,128)(2,1)S(1)}, bf16[64,1216]{1,0:T(8,128)(2,1)S(1)}, u32[]{:S(2)}, u32[]{:S(2)}) collective-permute-start(bf16[64,1216]{1,0:T(8,128)(2,1)S(1)} %multiply_convert_fusion.2), channel_id=1, source_target_pairs={{2,0},{3,1},{4,2},{5,3},{6,4},{7,5},{8,6},{9,7},{10,8},{11,9},{12,... | collective-permute-start | bytes 466952 | tf_op jit(solution)/shard_map/ppermute | solution.py:12
  156.5 5.3 %copy-start.26 = (bf16[64,1216]{1,0:T(8,128)(2,1)}, bf16[64,1216]{1,0:T(8,128)(2,1)S(1)}, u32[]{:S(2)}) copy-start(bf16[64,1216]{1,0:T(8,128)(2,1)S(1)} %collective-permute-done.24) | copy-start | bytes 466948
  156.5 34.2 %collective-permute-start.29 = (bf16[64,1216]{1,0:T(8,128)(2,1)S(1)}, bf16[64,1216]{1,0:T(8,128)(2,1)S(1)}, u32[]{:S(2)}, u32[]{:S(2)}) collective-permute-start(bf16[64,1216]{1,0:T(8,128)(2,1)S(1)} %multiply_convert_fusion.2), channel_id=1, source_target_pairs={{3,0},{4,1},{5,2},{6,3},{7,4},{8,5},{9,6},{10,7},{11,8},{12,9},{13... | collective-permute-start | bytes 466952 | tf_op jit(solution)/shard_map/ppermute | solution.py:12
  163.2 30.0 %collective-permute-start.30 = (bf16[64,1216]{1,0:T(8,128)(2,1)S(1)}, bf16[64,1216]{1,0:T(8,128)(2,1)S(1)}, u32[]{:S(2)}, u32[]{:S(2)}) collective-permute-start(bf16[64,1216]{1,0:T(8,128)(2,1)S(1)} %multiply_convert_fusion.2), channel_id=1, source_target_pairs={{4,0},{5,1},{6,2},{7,3},{8,4},{9,5},{10,6},{11,7},{12,8},{13,9},{1... | collective-permute-start | bytes 466952 | tf_op jit(solution)/shard_map/ppermute | solution.py:12
  169.2 9.5 %copy-start.28 = (bf16[64,1216]{1,0:T(8,128)(2,1)}, bf16[64,1216]{1,0:T(8,128)(2,1)S(1)}, u32[]{:S(2)}) copy-start(bf16[64,1216]{1,0:T(8,128)(2,1)S(1)} %collective-permute-done.26) | copy-start | bytes 466948
  169.2 30.1 %collective-permute-start.31 = (bf16[64,1216]{1,0:T(8,128)(2,1)S(1)}, bf16[64,1216]{1,0:T(8,128)(2,1)S(1)}, u32[]{:S(2)}, u32[]{:S(2)}) collective-permute-start(bf16[64,1216]{1,0:T(8,128)(2,1)S(1)} %multiply_convert_fusion.2), channel_id=1, source_target_pairs={{5,0},{6,1},{7,2},{8,3},{9,4},{10,5},{11,6},{12,7},{13,8},{14,9},{... | collective-permute-start | bytes 466952 | tf_op jit(solution)/shard_map/ppermute | solution.py:12
  178.9 20.6 %collective-permute-start.32 = (bf16[64,1216]{1,0:T(8,128)(2,1)S(1)}, bf16[64,1216]{1,0:T(8,128)(2,1)S(1)}, u32[]{:S(2)}, u32[]{:S(2)}) collective-permute-start(bf16[64,1216]{1,0:T(8,128)(2,1)S(1)} %multiply_convert_fusion.2), channel_id=1, source_target_pairs={{6,0},{7,1},{8,2},{9,3},{10,4},{11,5},{12,6},{13,7},{14,8},{15,9},... | collective-permute-start | bytes 466952 | tf_op jit(solution)/shard_map/ppermute | solution.py:12
  183.2 18.0 %collective-permute-start.33 = (bf16[64,1216]{1,0:T(8,128)(2,1)S(1)}, bf16[64,1216]{1,0:T(8,128)(2,1)S(1)}, u32[]{:S(2)}, u32[]{:S(2)}) collective-permute-start(bf16[64,1216]{1,0:T(8,128)(2,1)S(1)} %multiply_convert_fusion.2), channel_id=1, source_target_pairs={{7,0},{8,1},{9,2},{10,3},{11,4},{12,5},{13,6},{14,7},{15,8},{16,9}... | collective-permute-start | bytes 466952 | tf_op jit(solution)/shard_map/ppermute | solution.py:12
  190.7 19.5 %collective-permute-start.34 = (bf16[64,1216]{1,0:T(8,128)(2,1)S(1)}, bf16[64,1216]{1,0:T(8,128)(2,1)S(1)}, u32[]{:S(2)}, u32[]{:S(2)}) collective-permute-start(bf16[64,1216]{1,0:T(8,128)(2,1)S(1)} %multiply_convert_fusion.2), channel_id=1, source_target_pairs={{8,0},{9,1},{10,2},{11,3},{12,4},{13,5},{14,6},{15,7},{16,8},{17,9... | collective-permute-start | bytes 466952 | tf_op jit(solution)/shard_map/ppermute | solution.py:12
  193.2 17.6 %collective-permute-start.35 = (bf16[64,1216]{1,0:T(8,128)(2,1)S(1)}, bf16[64,1216]{1,0:T(8,128)(2,1)S(1)}, u32[]{:S(2)}, u32[]{:S(2)}) collective-permute-start(bf16[64,1216]{1,0:T(8,128)(2,1)S(1)} %multiply_convert_fusion.2), channel_id=1, source_target_pairs={{9,0},{10,1},{11,2},{12,3},{13,4},{14,5},{15,6},{16,7},{17,8},{18,... | collective-permute-start | bytes 466952 | tf_op jit(solution)/shard_map/ppermute | solution.py:12
  201.3 9.0 %copy-start.10 = (bf16[64,1216]{1,0:T(8,128)(2,1)}, bf16[64,1216]{1,0:T(8,128)(2,1)S(1)}, u32[]{:S(2)}) copy-start(bf16[64,1216]{1,0:T(8,128)(2,1)S(1)} %collective-permute-done.33) | copy-start | bytes 466948
  (37 other events, 42.3 us)
where the time goes:
time: 229 us; the launch traced here: 227 us
  starting transfers between devices  157 us (69%)
  local copies, waits for them, and re-layouts  24.5 us (11%)
  matrix products  21.8 us (10%)
  waiting for transfers between devices  19.1 us (8%)
    ppermute x36, starting transfers between devices, from_behind(): lax.ppermute(value, axis, [(source, source + steps) for source in range(f...  157 us
    unnamed x152, local copies, waits for them, and re-layouts  22.1 us
    dot_general x76, matrix products, band_product(): jnp.einsum('iax,ibx->iab', left_part, right_part, preferred_element_type=...  21.8 us
    ppermute x36, waiting for transfers between devices, from_behind(): lax.ppermute(value, axis, [(source, source + steps) for source in range(f...  19.1 us
  transfers between devices with their start and end apart: 36, of which 6 were waited for; matrix products, arithmetic and copies ran while one was open for 6% of the time, Pallas kernels for 0%

commit v1 on v0

v1 whole, which is shorter than its diff:
```python
import functools

import jax
import jax.numpy as jnp
from jax import lax
from jax.experimental import pallas as pl
from jax.experimental.pallas import tpu as pltpu
from jax.sharding import PartitionSpec as P

STEPS = 2
BLOCK = 64
HALF = 9
SLOTS = 2 * HALF + 1
LANES = 128
TILES = 10
WIDTH = TILES * LANES
FULL = SLOTS * BLOCK
STORED = 13
LINE = 8
EVENS = 9 * BLOCK
ODDS = 10 * BLOCK
MESH = pl.DeviceIdType.MESH


def offset_of(d):
    return (d + 1) // 2


def rows_of(step, d):
    order = (d + HALF - 1) // 2 if d % 2 == 0 else HALF + (d + HALF) // 2
    return pl.ds(step * FULL + order * BLOCK, BLOCK)


def needed_tiles(d):
    if d > 0:
        return 0, (2 * HALF - d) // 2
    return (-d) // 2, TILES - 1


ROUTES = []
for near in (1, 2, 3, 4):
    ROUTES.append((-near, 1, 1 - near))
    ROUTES.append((near, -1, near - 1))
for far in (5, 6, 7, 8, 9):
    ROUTES.append((-far, LINE, LINE - far))
    ROUTES.append((far, -LINE, far - LINE))


def tiles_sent(d):
    if abs(d) <= 3:
        return 0, TILES - 1
    return needed_tiles(d)


def kernel(total, columns, dens_ref, pat_ref, out_ref, band, shifted, squares, low, send_sem, recv_sem):
    me = lax.axis_index("row") * columns + lax.axis_index("col")

    def place(index):
        return (index // columns, lax.rem(index, columns))

    def copy(step, d, delta, source):
        first, last = tiles_sent(d)
        there = me + delta
        span = (last - first + 1) * LANES
        return pltpu.make_async_remote_copy(
            src_ref=band.at[rows_of(step, source), pl.ds((1 + first + offset_of(source)) * LANES, span)],
            dst_ref=band.at[rows_of(step, d), pl.ds((1 + first + offset_of(d)) * LANES, span)],
            send_sem=send_sem.at[step, d + HALF],
            recv_sem=recv_sem.at[step, d + HALF],
            device_id=place(there),
            device_id_type=MESH,
        )

    def inside(index):
        return (index >= 0) & (index < total)


    def edge_target(d):
        there = me - d
        if d < 0:
            return (there < LINE) & (there < total)
        return (there >= total - LINE) & (there >= 0)

    def edge_source(d):
        if d < 0:
            return (me < LINE) & (me + d >= 0)
        return (me >= total - LINE) & (me + d < total)

    EDGES = [d for far in (5, 6, 7) for d in (-far, far)]

    for step in range(STEPS):
        for d in range(-HALF, HALF + 1):
            if d == 0:
                continue
            off = offset_of(d)
            if d > 0:
                band[rows_of(step, d), LANES:(1 + off) * LANES] = jnp.zeros((BLOCK, off * LANES), jnp.bfloat16)
            elif off < 0:
                band[rows_of(step, d), (1 + TILES + off) * LANES:(1 + TILES) * LANES] = jnp.zeros((BLOCK, -off * LANES), jnp.bfloat16)

            @pl.when(jnp.logical_not(inside(me + d)))
            def _():
                band[rows_of(step, d), LANES:(1 + TILES) * LANES] = jnp.zeros((BLOCK, WIDTH), jnp.bfloat16)

    barrier = pltpu.get_barrier_semaphore()
    count = jnp.int32(0)
    for delta in (-LINE, -1, 1, LINE):
        there = me + delta

        @pl.when(inside(there))
        def _():
            pl.semaphore_signal(barrier, inc=1, device_id=place(there), device_id_type=MESH)

        count += inside(there).astype(jnp.int32)
    for d in EDGES:
        @pl.when(edge_target(d))
        def _():
            pl.semaphore_signal(barrier, inc=1, device_id=place(me - d), device_id_type=MESH)

        @pl.when(edge_source(d))
        def _():
            pl.semaphore_signal(barrier, inc=1, device_id=place(me + d), device_id_type=MESH)

        count += edge_target(d).astype(jnp.int32) + edge_source(d).astype(jnp.int32)
    pl.semaphore_wait(barrier, count)

    low[0:BLOCK, :] = jnp.zeros((BLOCK, BLOCK), jnp.bfloat16)
    low[(SLOTS + 1) * BLOCK:(SLOTS + 2) * BLOCK, :] = jnp.zeros((BLOCK, BLOCK), jnp.bfloat16)
    squares[(SLOTS + 1) * BLOCK:(SLOTS + 2) * BLOCK, :] = jnp.zeros((BLOCK, BLOCK), jnp.float32)
    squares[0:BLOCK, :] = jnp.zeros((BLOCK, BLOCK), jnp.float32)

    def forward(step, source):
        for d, delta, from_slot in ROUTES:
            if from_slot == source:
                @pl.when(inside(me + delta) & inside(me + source))
                def _():
                    copy(step, d, delta, source).start()

    def has_route(d):
        delta = [entry[1] for entry in ROUTES if entry[0] == d][0]
        return inside(me + d) & inside(me - delta)

    def wait_for(step, d):
        present = has_route(d)
        if d in EDGES:
            present = present | edge_source(d)

        @pl.when(present)
        def _():
            copy(step, d, 0, 0).wait_recv()

    for step in range(STEPS):
        own = rows_of(step, 0)
        if step == 0:
            current = dens_ref[...]
            band[own, LANES:LANES + FULL] = current.astype(jnp.bfloat16)
            band[own, LANES + FULL:LANES + WIDTH] = jnp.zeros((BLOCK, WIDTH - FULL), jnp.bfloat16)
        else:
            for tile in range(TILES):
                part = squares[(1 + 2 * tile) * BLOCK:(3 + 2 * tile) * BLOCK, :]
                band[own, (1 + tile) * LANES:(2 + tile) * LANES] = part.T.astype(jnp.bfloat16)
        forward(step, 0)
        for d in EDGES:
            @pl.when(edge_target(d))
            def _():
                copy(step, d, -d, 0).start()
        if step == 0:
            padded = jnp.concatenate([jnp.zeros((BLOCK, BLOCK), jnp.float32), current], axis=1)
            shifted[...] = padded.astype(jnp.bfloat16)
        else:
            for tile in range(TILES):
                part = squares[2 * tile * BLOCK:(2 + 2 * tile) * BLOCK, :]
                shifted[:, tile * LANES:(1 + tile) * LANES] = part.T.astype(jnp.bfloat16)
        for near in (1, 2, 3):
            for d in (-near, near):
                wait_for(step, d)
                forward(step, d)
        for near in (4, 5, 6, 7, 8, 9):
            for d in (-near, near):
                wait_for(step, d)
        window = slice(LANES, LANES + WIDTH)
        even_rows = band[pl.ds(step * FULL, EVENS), window]
        odd_rows = band[pl.ds(step * FULL + EVENS, ODDS), window]
        across = (((1,), (1,)), ((), ()))
        even_square = lax.dot_general(even_rows, band[own, window], across, preferred_element_type=jnp.float32)
        odd_square = lax.dot_general(odd_rows, shifted[...], across, preferred_element_type=jnp.float32)
        for slot in range(SLOTS):
            order = (slot - 1) // 2 if slot % 2 else slot // 2
            source = even_square if slot % 2 else odd_square
            kept = pat_ref[0, slot].astype(jnp.float32)
            part = source[order * BLOCK:(order + 1) * BLOCK, :] * kept
            squares[(1 + slot) * BLOCK:(2 + slot) * BLOCK, :] = part
            low[(1 + slot) * BLOCK:(2 + slot) * BLOCK, :] = part.astype(jnp.bfloat16)
        even_cube = jnp.dot(even_rows, low[BLOCK:BLOCK + WIDTH, :], preferred_element_type=jnp.float32)
        odd_cube = jnp.dot(odd_rows, low[0:WIDTH, :], preferred_element_type=jnp.float32)
        for slot in range(SLOTS):
            order = (slot - 1) // 2 if slot % 2 else slot // 2
            source = even_cube if slot % 2 else odd_cube
            kept = pat_ref[0, slot].astype(jnp.float32)
            part = squares[(1 + slot) * BLOCK:(2 + slot) * BLOCK, :]
            cube = source[order * BLOCK:(order + 1) * BLOCK, :]
            squares[(1 + slot) * BLOCK:(2 + slot) * BLOCK, :] = (3.0 * part - 2.0 * cube) * kept

    for tile in range(TILES):
        part = squares[(1 + 2 * tile) * BLOCK:(3 + 2 * tile) * BLOCK, :].T
        wide = min(LANES, FULL - tile * LANES)
        out_ref[:, tile * LANES:tile * LANES + wide] = part[:, :wide]

    for step in range(STEPS):
        for d, delta, source in ROUTES:
            @pl.when(inside(me + delta) & inside(me + source))
            def _():
                copy(step, d, delta, source).wait_send()
        for d in EDGES:
            @pl.when(edge_target(d))
            def _():
                copy(step, d, -d, 0).wait_send()


def solution(mesh):
    columns = mesh.shape["col"]
    total = mesh.shape["row"] * columns

    def local(density, pattern):
        return pl.pallas_call(
            functools.partial(kernel, total, columns),
            out_shape=jax.ShapeDtypeStruct((BLOCK, FULL), jnp.float32),
            in_specs=[
                pl.BlockSpec(memory_space=pltpu.VMEM),
                pl.BlockSpec(memory_space=pltpu.SMEM),
            ],
            out_specs=pl.BlockSpec(memory_space=pltpu.VMEM),
            scratch_shapes=[
                pltpu.VMEM((STEPS * FULL, STORED * LANES), jnp.bfloat16),
                pltpu.VMEM((BLOCK, WIDTH), jnp.bfloat16),
                pltpu.VMEM(((SLOTS + 2) * BLOCK, BLOCK), jnp.float32),
                pltpu.VMEM(((SLOTS + 2) * BLOCK, BLOCK), jnp.bfloat16),
                pltpu.SemaphoreType.DMA((STEPS, SLOTS)),
                pltpu.SemaphoreType.DMA((STEPS, SLOTS)),
            ],
            compiler_params=pltpu.CompilerParams(
                collective_id=0, has_side_effects=True, vmem_limit_bytes=40 << 20
            ),
        )(density, pattern)

    placed = (P(("row", "col"), None), P(("row", "col"), None))
    return jax.shard_map(
        local, mesh=mesh, in_specs=placed, out_specs=P(("row", "col"), None), check_vma=False
    )
```

time: 229 us -> 73.8 us (0.32)
  the two profiles are of different devices: /device:TPU:61 before, /device:TPU:1 now
where the time goes in v1:
time: 73.8 us; the launch traced here: 72.9 us
  Pallas kernels  70.6 us (96%)
  local copies, waits for them, and re-layouts  2.35 us (3%)
    pallas_call x1, Pallas kernels, local(): pl.pallas_call(functools.partial(kernel, total, columns), out_shape=jax.S...  70.6 us
    unnamed x5, local copies, waits for them, and re-layouts  2.35 us

profile of v1, /device:TPU:1, one launch (start us, length us, event | category | flops | bytes accessed | tf_op | source)
XLA Modules:
  0.0 72.9 jit_solution(1089801698418459745)
XLA Ops:
  0.0 0.0 copy-start
  0.0 1.0 %copy-done = f32[64,1216]{1,0:T(8,128)S(1)} copy-done((f32[64,1216]{1,0:T(8,128)S(1)}, f32[64,1216]{1,0:T(8,128)}, u32[]{:S(2)}) %copy-start) | copy-done | bytes 311320
  1.0 0.0 copy-start.1
  1.0 0.7 copy-done.1
  1.6 70.6 %shard_map.28 = f32[64,1216]{1,0:T(8,128)S(1)} custom-call(f32[64,1216]{1,0:T(8,128)S(1)} %copy-done, s32[1,19]{1,0:T(1,128)S(1)} %copy-done.1), custom_call_target="tpu_custom_call" | custom-call | tf_op jit(solution)/shard_map/pallas_call | solution.py:225
  72.2 0.7 copy.4
Async XLA Ops:
  0.0 1.0 %copy-start = (f32[64,1216]{1,0:T(8,128)S(1)}, f32[64,1216]{1,0:T(8,128)}, u32[]{:S(2)}) copy-start(f32[64,1216]{1,0:T(8,128)} %dens_ref.1) | copy-start | bytes 933892
  1.0 0.7 copy-start.1

commit v2 on v1

v2 whole, which is shorter than its diff:
```python
import functools

import jax
import jax.numpy as jnp
from jax import lax
from jax.experimental import pallas as pl
from jax.experimental.pallas import tpu as pltpu
from jax.sharding import PartitionSpec as P

STEPS = 2
BLOCK = 64
HALF = 9
SLOTS = 2 * HALF + 1
LANES = 128
TILES = 10
WIDTH = TILES * LANES
FULL = SLOTS * BLOCK
LINE = 8
EVENS = 9 * BLOCK
ODDS = 10 * BLOCK
MARGIN = 4
STORED = TILES + 9
CUT = 5
PARTS = ((0, CUT - 1), (CUT, TILES - 1))
MESH = pl.DeviceIdType.MESH

ROUTES = (
    ((8, 1, 1, 0), (-8, 0, -1, 0), (7, 1, 0, 7), (1, 0, 0, 1), (8, 0, 1, 0), (-8, 1, -1, 0), (7, 0, 0, 7),
     (1, 1, 0, 1), (-7, 0, 0, 1), (-9, 0, -1, 7), (-1, 1, -1, 0), (2, 0, 0, 1), (6, 0, 0, 7), (9, 0, 1, 0),
     (6, 1, 0, 7), (-1, 0, -1, 0), (-7, 1, 0, 1), (2, 1, 0, 1), (5, 1, 0, 7), (-9, 1, -1, 0), (-6, 0, -1, 0),
     (-2, 0, -1, 0), (4, 1, 0, 6), (-2, 1, 0, 7), (-6, 1, -1, 0), (4, 0, 0, 1), (5, 0, 0, 7), (-5, 0, 0, 1),
     (-3, 1, -1, 0), (3, 0, 0, 7), (-4, 0, 0, 1), (-4, 1, -1, 0), (3, 1, 0, 7), (-5, 1, 0, 1), (-3, 0, -1, 0)),
    ((-8, 0, -1, 1), (1, 0, 0, 2), (-1, 0, 0, 0), (8, 0, 1, 1), (8, 1, 1, 1), (-8, 1, -1, 1), (1, 1, 0, 2),
     (-1, 1, 0, 0), (7, 1, 0, 0), (-7, 0, 0, 2), (-9, 0, -1, 0), (6, 1, 0, 0), (9, 0, 1, 1), (2, 0, 0, 2),
     (-7, 1, -1, 1), (6, 0, 0, 0), (7, 0, 1, 1), (2, 1, 0, 2), (-9, 1, -1, 1), (3, 0, 0, 2), (5, 0, 0, 0),
     (-2, 1, -1, 1), (-6, 0, -1, 1), (-4, 0, 0, 4), (3, 1, 0, 2), (-2, 0, 0, 0), (-5, 0, -1, 1), (-6, 1, 0, 2),
     (4, 1, 0, 0), (-3, 0, 0, 0), (4, 0, 0, 2), (5, 1, 0, 2), (-5, 1, -1, 1), (-3, 1, 0, 0), (-4, 1, -1, 1)),
    ((-8, 0, -1, 2), (-1, 1, 0, 1), (1, 0, 0, 3), (8, 0, 1, 2), (8, 1, 1, 2), (-8, 1, -1, 2), (-1, 0, 0, 1),
     (1, 1, 0, 3), (-7, 0, -1, 3), (2, 0, 0, 3), (-9, 1, -1, 2), (-2, 0, 0, 1), (9, 0, 1, 2), (-9, 0, -1, 2),
     (2, 1, 0, 3), (-2, 1, 0, 1), (7, 0, 1, 2), (-7, 1, -1, 2), (-6, 0, -1, 2), (5, 1, 0, 1), (3, 0, 0, 3),
     (6, 0, 1, 2), (6, 1, 1, 2), (-6, 1, -1, 2), (4, 1, 0, 0), (3, 1, 0, 3), (7, 1, 0, 3), (5, 0, 0, 1),
     (-3, 1, -1, 2), (-5, 0, -1, 2), (4, 0, 0, 1), (-5, 1, 0, 3), (-3, 0, 0, 1), (-4, 1, -1, 3), (-4, 0, 0, 3)),
    ((8, 1, 1, 3), (-8, 0, -1, 3), (1, 0, 0, 4), (-1, 0, 0, 2), (8, 0, 1, 3), (-8, 1, -1, 3), (1, 1, 0, 4),
     (-1, 1, 0, 2), (-7, 0, 0, 4), (-2, 1, 0, 2), (9, 0, 1, 3), (2, 0, 0, 4), (-2, 0, 0, 2), (-7, 1, -1, 3),
     (7, 0, 1, 3), (2, 1, 0, 4), (-9, 0, 0, 1), (7, 1, 1, 3), (-9, 1, -1, 3), (6, 1, 1, 3), (3, 0, 0, 4),
     (-6, 0, -1, 3), (-3, 0, 0, 2), (6, 0, 1, 3), (-6, 1, -1, 3), (-3, 1, 0, 2), (3, 1, 0, 4), (-5, 0, -1, 3),
     (4, 0, 0, 4), (4, 1, 0, 4), (5, 0, 0, 2), (5, 1, 0, 2), (-5, 1, 0, 4), (-4, 0, -1, 2), (-4, 1, 0, 2)),
    ((-8, 0, -1, 4), (-1, 1, 0, 3), (1, 0, 0, 5), (8, 0, 1, 4), (8, 1, 1, 4), (-8, 1, -1, 4), (-1, 0, 0, 3),
     (1, 1, 0, 5), (7, 1, 0, 3), (2, 0, 0, 5), (-9, 1, -1, 4), (-2, 0, 0, 3), (9, 0, 1, 4), (-7, 0, -1, 4),
     (-9, 0, -1, 4), (2, 1, 0, 5), (-2, 1, 0, 3), (7, 0, 1, 4), (-7, 1, -1, 4), (-6, 0, -1, 4), (-3, 1, 0, 3),
     (3, 0, 0, 5), (6, 0, 1, 4), (6, 1, 1, 4), (3, 1, 0, 5), (-6, 1, -1, 4), (-3, 0, 0, 3), (5, 1, 1, 4),
     (-5, 0, 0, 5), (-4, 0, 0, 3), (-5, 1, 0, 5), (5, 0, 0, 3), (4, 1, 1, 5), (-4, 1, 0, 3), (4, 0, 0, 5)),
    ((-8, 0, -1, 5), (8, 1, 1, 5), (1, 0, 0, 6), (-1, 0, 0, 4), (-8, 1, -1, 5), (1, 1, 0, 6), (-1, 1, 0, 4),
     (7, 1, 1, 4), (8, 0, 1, 5), (-2, 1, 0, 4), (2, 0, 0, 6), (9, 0, 1, 5), (-2, 0, 0, 4), (-7, 1, -1, 5),
     (2, 1, 0, 6), (7, 0, 1, 5), (-9, 1, -1, 5), (-4, 0, 0, 7), (6, 1, 1, 5), (-3, 0, 0, 4), (-6, 0, -1, 5),
     (-5, 0, 0, 6), (6, 0, 1, 5), (-3, 1, 0, 4), (-6, 1, -1, 5), (-5, 1, 0, 6), (-7, 0, 0, 4), (3, 1, 0, 6),
     (3, 0, 1, 5), (5, 0, 0, 4), (-9, 0, -1, 1), (-4, 1, 0, 6), (4, 0, 1, 4), (5, 1, 1, 5), (4, 1, 0, 4)),
    ((-8, 0, -1, 6), (-1, 1, 0, 5), (1, 0, 0, 7), (8, 0, 1, 6), (8, 1, 1, 6), (-8, 1, -1, 6), (-1, 0, 0, 5),
     (1, 1, 0, 7), (-9, 0, 0, 5), (7, 1, 0, 5), (-7, 0, 0, 7), (-2, 0, 0, 5), (-9, 1, -1, 6), (-6, 0, 0, 7),
     (9, 0, 1, 6), (-2, 1, 0, 5), (-6, 1, 0, 7), (-7, 1, -1, 6), (7, 0, 1, 6), (-3, 1, 0, 5), (2, 0, 1, 6),
     (2, 1, 0, 7), (6, 1, 1, 6), (-3, 0, 0, 5), (-5, 1, 0, 7), (5, 1, 1, 6), (4, 1, 0, 3), (-4, 0, 0, 7), (6, 0, 0, 5),
     (3, 1, 0, 7), (-5, 0, 0, 5), (5, 0, 1, 6), (-4, 1, 0, 5), (3, 0, 0, 7), (4, 0, 1, 6)),
    ((-8, 0, -1, 7), (-7, 0, 0, 0), (-1, 0, 0, 6), (8, 0, 1, 7), (8, 1, 1, 7), (-7, 1, 0, 0), (-1, 1, 0, 6),
     (-9, 0, -1, 6), (-6, 0, 0, 0), (-8, 1, -1, 7), (-2, 1, 0, 6), (1, 0, 1, 7), (1, 1, 1, 7), (7, 0, 0, 6),
     (-6, 1, 0, 0), (7, 1, 0, 6), (-9, 1, -1, 7), (6, 1, 1, 7), (-2, 0, 0, 6), (-5, 0, 0, 0), (9, 0, 1, 7),
     (2, 1, 1, 7), (-4, 0, 0, 1), (2, 0, 0, 0), (6, 0, 1, 7), (-4, 1, 0, 6), (5, 1, 0, 6), (-5, 1, 0, 0), (3, 0, 1, 7),
     (4, 1, 0, 6), (-3, 1, 0, 0), (4, 0, 1, 7), (-3, 0, 0, 0), (3, 1, 1, 7), (5, 0, 0, 6)),
)


def offset_of(d):
    return (d + 1) // 2


def line_of(y, d):
    return (y + d) // LINE


def needed_tiles(d, part):
    first, last = (0, (2 * HALF - d) // 2) if d > 0 else ((-d) // 2, TILES - 1)
    return max(first, PARTS[part][0]), min(last, PARTS[part][1])


def source_slot(y, d, line, column):
    return d + y - line * LINE - column


def receivers(column, slot, part):
    found = []
    for y in range(LINE):
        for d, piece, line, relay in ROUTES[y]:
            if relay == column and piece == part and source_slot(y, d, line, relay) == slot:
                found.append((y, d, -line))
    return found


@functools.cache
def sent_tiles(y, d, part):
    first, last = needed_tiles(d, part)
    for y_next, d_next, _ in receivers(y, d, part):
        first_next, last_next = sent_tiles(y_next, d_next, part)
        first, last = min(first, first_next), max(last, last_next)
    return first, last


@functools.cache
def depth_of(y, d, part):
    return 1 + max([depth_of(y_next, d_next, part) for y_next, d_next, _ in receivers(y, d, part)], default=0)


def sends_from(column):
    own = [(0, part, *entry) for part in range(2) for entry in receivers(column, 0, part)]
    own.sort(key=lambda entry: -depth_of(entry[2], entry[3], entry[1]))
    relayed = [
        (d, part, *entry) for d, part, _, _ in ROUTES[column] for entry in receivers(column, d, part)
    ]
    return own + relayed


MOST_SENDS = max(len(sends_from(column)) for column in range(LINE))


def partners_of(column):
    found = {(line, relay) for _, _, line, relay in ROUTES[column]}
    return sorted(found | {(line, y) for _, _, y, _, line in sends_from(column)})


def kernel(lines, columns, dens_ref, pat_ref, out_ref, band, shifted, squares, low, send_sem, recv_sem):
    me = lax.axis_index("row") * columns + lax.axis_index("col")
    my_line = me // LINE
    my_column = lax.rem(me, LINE)

    def place(line, y):
        index = (my_line + line) * LINE + y
        return (index // columns, lax.rem(index, columns))

    there = {line: (my_line + line >= 0) & (my_line + line < lines) for line in range(-2, 3)}

    def rows_of(step, d):
        order = (d + HALF - 1) // 2 if d % 2 == 0 else HALF + (d + HALF) // 2
        return pl.ds(pl.multiple_of(step * FULL + order * BLOCK, BLOCK), BLOCK)

    def lanes_of(d, first, last):
        return pl.ds((MARGIN + offset_of(d) + first) * LANES, (last - first + 1) * LANES)

    def copy(step, number, slot, part, y, d, line):
        first, last = sent_tiles(y, d, part)
        return pltpu.make_async_remote_copy(
            src_ref=band.at[rows_of(step, slot), lanes_of(slot, first, last)],
            dst_ref=band.at[rows_of(step, d), lanes_of(d, first, last)],
            send_sem=send_sem.at[step, number],
            recv_sem=recv_sem.at[step, 2 * (d + HALF) + part],
            device_id=place(line, y),
            device_id_type=MESH,
        )

    def arrival(step, y, d, part):
        first, last = sent_tiles(y, d, part)
        piece = band.at[rows_of(step, d), lanes_of(d, first, last)]
        return pltpu.make_async_remote_copy(
            src_ref=piece,
            dst_ref=piece,
            send_sem=send_sem.at[step, 0],
            recv_sem=recv_sem.at[step, 2 * (d + HALF) + part],
            device_id=place(0, y),
            device_id_type=MESH,
        )

    def each_column(body):
        for column in range(LINE):
            pl.when(my_column == column)(functools.partial(body, column))

    def sent_when(column, slot, line):
        return there[line] & there[line_of(column, slot)]

    for step in range(STEPS):
        for d in range(-HALF, HALF + 1):
            off = offset_of(d)
            if d > 0:
                band[rows_of(step, d), MARGIN * LANES:(MARGIN + off) * LANES] = jnp.zeros(
                    (BLOCK, off * LANES), jnp.bfloat16
                )
            elif off < 0:
                band[rows_of(step, d), (MARGIN + TILES + off) * LANES:(MARGIN + TILES) * LANES] = jnp.zeros(
                    (BLOCK, -off * LANES), jnp.bfloat16
                )
            if d != 0:
                @pl.when((me + d < 0) | (me + d >= lines * LINE))
                def _():
                    band[rows_of(step, d), MARGIN * LANES:(MARGIN + TILES) * LANES] = jnp.zeros(
                        (BLOCK, WIDTH), jnp.bfloat16
                    )

    barrier = pltpu.get_barrier_semaphore()

    def greet(column):
        count = jnp.int32(0)
        for line, y in partners_of(column):
            @pl.when(there[line])
            def _():
                pl.semaphore_signal(barrier, inc=1, device_id=place(line, y), device_id_type=MESH)

            count += there[line].astype(jnp.int32)
        pl.semaphore_wait(barrier, count)

    each_column(greet)

    low[0:BLOCK, :] = jnp.zeros((BLOCK, BLOCK), jnp.bfloat16)
    low[(SLOTS + 1) * BLOCK:(SLOTS + 2) * BLOCK, :] = jnp.zeros((BLOCK, BLOCK), jnp.bfloat16)
    squares[(SLOTS + 1) * BLOCK:(SLOTS + 2) * BLOCK, :] = jnp.zeros((BLOCK, BLOCK), jnp.float32)
    squares[0:BLOCK, :] = jnp.zeros((BLOCK, BLOCK), jnp.float32)

    current = dens_ref[...]
    padded = jnp.concatenate(
        [current, jnp.zeros((BLOCK, WIDTH - FULL), jnp.float32)], axis=1
    )
    band[rows_of(0, 0), MARGIN * LANES:(MARGIN + TILES) * LANES] = padded.astype(jnp.bfloat16)
    padded = jnp.concatenate([jnp.zeros((BLOCK, BLOCK), jnp.float32), current], axis=1)
    shifted[...] = padded.astype(jnp.bfloat16)
    window = pl.ds(MARGIN * LANES, WIDTH)

    def purify(step, _):
        def exchange(column):
            sends = sends_from(column)

            def send(slot, part):
                for number, entry in enumerate(sends):
                    if entry[:2] == (slot, part):
                        @pl.when(sent_when(column, slot, entry[4]))
                        def _():
                            copy(step, number, *entry).start()

            for number, entry in enumerate(sends):
                if entry[0] == 0:
                    @pl.when(sent_when(column, 0, entry[4]))
                    def _():
                        copy(step, number, *entry).start()
            for d, part, _, _ in ROUTES[column]:
                @pl.when(there[line_of(column, d)])
                def _():
                    arrival(step, column, d, part).wait_recv()

                send(d, part)

        each_column(exchange)
        own = band[rows_of(step, 0), window]
        even_rows = band[pl.ds(pl.multiple_of(step * FULL, BLOCK), EVENS), window]
        odd_rows = band[pl.ds(pl.multiple_of(step * FULL + EVENS, BLOCK), ODDS), window]
        across = (((1,), (1,)), ((), ()))
        even_square = lax.dot_general(even_rows, own, across, preferred_element_type=jnp.float32)
        odd_square = lax.dot_general(odd_rows, shifted[...], across, preferred_element_type=jnp.float32)
        for slot in range(SLOTS):
            order = (slot - 1) // 2 if slot % 2 else slot // 2
            source = even_square if slot % 2 else odd_square
            kept = pat_ref[0, slot].astype(jnp.float32)
            part = source[order * BLOCK:(order + 1) * BLOCK, :] * kept
            squares[(1 + slot) * BLOCK:(2 + slot) * BLOCK, :] = part
            low[(1 + slot) * BLOCK:(2 + slot) * BLOCK, :] = part.astype(jnp.bfloat16)
        even_cube = jnp.dot(even_rows, low[BLOCK:BLOCK + WIDTH, :], preferred_element_type=jnp.float32)
        odd_cube = jnp.dot(odd_rows, low[0:WIDTH, :], preferred_element_type=jnp.float32)
        for slot in range(SLOTS):
            order = (slot - 1) // 2 if slot % 2 else slot // 2
            source = even_cube if slot % 2 else odd_cube
            kept = pat_ref[0, slot].astype(jnp.float32)
            part = squares[(1 + slot) * BLOCK:(2 + slot) * BLOCK, :]
            cube = source[order * BLOCK:(order + 1) * BLOCK, :]
            squares[(1 + slot) * BLOCK:(2 + slot) * BLOCK, :] = (3.0 * part - 2.0 * cube) * kept

        @pl.when(step < STEPS - 1)
        def _():
            for tile in range(TILES):
                part = squares[(1 + 2 * tile) * BLOCK:(3 + 2 * tile) * BLOCK, :]
                band[rows_of(step + 1, 0), (MARGIN + tile) * LANES:(MARGIN + 1 + tile) * LANES] = part.T.astype(
                    jnp.bfloat16
                )
            for tile in range(TILES):
                part = squares[2 * tile * BLOCK:(2 + 2 * tile) * BLOCK, :]
                shifted[:, tile * LANES:(1 + tile) * LANES] = part.T.astype(jnp.bfloat16)

        return 0

    lax.fori_loop(0, STEPS, purify, 0)

    for tile in range(TILES):
        part = squares[(1 + 2 * tile) * BLOCK:(3 + 2 * tile) * BLOCK, :].T
        wide = min(LANES, FULL - tile * LANES)
        out_ref[:, tile * LANES:tile * LANES + wide] = part[:, :wide]

    def finish(step, _):
        def drain(column):
            for number, entry in enumerate(sends_from(column)):
                @pl.when(sent_when(column, entry[0], entry[4]))
                def _():
                    copy(step, number, *entry).wait_send()

        each_column(drain)
        return 0

    lax.fori_loop(0, STEPS, finish, 0)


def solution(mesh):
    columns = mesh.shape["col"]
    lines = mesh.shape["row"] * columns // LINE

    def local(density, pattern):
        return pl.pallas_call(
            functools.partial(kernel, lines, columns),
            out_shape=jax.ShapeDtypeStruct((BLOCK, FULL), jnp.float32),
            in_specs=[
                pl.BlockSpec(memory_space=pltpu.VMEM),
                pl.BlockSpec(memory_space=pltpu.SMEM),
            ],
            out_specs=pl.BlockSpec(memory_space=pltpu.VMEM),
            scratch_shapes=[
                pltpu.VMEM((STEPS * FULL, STORED * LANES), jnp.bfloat16),
                pltpu.VMEM((BLOCK, WIDTH), jnp.bfloat16),
                pltpu.VMEM(((SLOTS + 2) * BLOCK, BLOCK), jnp.float32),
                pltpu.VMEM(((SLOTS + 2) * BLOCK, BLOCK), jnp.bfloat16),
                pltpu.SemaphoreType.DMA((STEPS, MOST_SENDS)),
                pltpu.SemaphoreType.DMA((STEPS, 2 * SLOTS)),
            ],
            compiler_params=pltpu.CompilerParams(
                collective_id=0, has_side_effects=True, vmem_limit_bytes=40 << 20
            ),
        )(density, pattern)

    placed = (P(("row", "col"), None), P(("row", "col"), None))
    return jax.shard_map(
        local, mesh=mesh, in_specs=placed, out_specs=P(("row", "col"), None), check_vma=False
    )
```

time: 73.8 us -> 67.6 us (0.916); the launches traced: 72.9 us -> 67.5 us
  Pallas kernels: 70.6 us -> 65.1 us
    pallas_call x1, Pallas kernels: 70.6 us -> 65.1 us  [local(): pl.pallas_call(functools.partial(kernel, lines, columns), out_shape=jax.S...]
where the time goes in v2:
time: 67.6 us; the launch traced here: 67.5 us
  Pallas kernels  65.1 us (96%)
  local copies, waits for them, and re-layouts  2.35 us (3%)
    pallas_call x1, Pallas kernels, local(): pl.pallas_call(functools.partial(kernel, lines, columns), out_shape=jax.S...  65.1 us
    unnamed x5, local copies, waits for them, and re-layouts  2.35 us

profile of v2, /device:TPU:1, one launch (start us, length us, event | category | flops | bytes accessed | tf_op | source)
XLA Modules:
  0.0 67.5 jit_solution(8454631357571711737)
XLA Ops:
  0.0 0.0 copy-start
  0.0 1.0 %copy-done = f32[64,1216]{1,0:T(8,128)S(1)} copy-done((f32[64,1216]{1,0:T(8,128)S(1)}, f32[64,1216]{1,0:T(8,128)}, u32[]{:S(2)}) %copy-start) | copy-done | bytes 311320
  1.0 0.0 copy-start.1
  1.0 0.7 copy-done.1
  1.6 65.1 %shard_map.28 = f32[64,1216]{1,0:T(8,128)S(1)} custom-call(f32[64,1216]{1,0:T(8,128)S(1)} %copy-done, s32[1,19]{1,0:T(1,128)S(1)} %copy-done.1), custom_call_target="tpu_custom_call" | custom-call | tf_op jit(solution)/shard_map/pallas_call | solution.py:307
  66.7 0.7 %copy.4 = f32[64,1216]{1,0:T(8,128)} copy(f32[64,1216]{1,0:T(8,128)S(1)} %shard_map.28) | data formatting | bytes 622592
Async XLA Ops:
  0.0 1.0 %copy-start = (f32[64,1216]{1,0:T(8,128)S(1)}, f32[64,1216]{1,0:T(8,128)}, u32[]{:S(2)}) copy-start(f32[64,1216]{1,0:T(8,128)} %dens_ref.1) | copy-start | bytes 933892
  1.0 0.7 copy-start.1

commit v3 on v2

v3 whole, which is shorter than its diff:
```python
import functools

import jax
import jax.numpy as jnp
from jax import lax
from jax.experimental import pallas as pl
from jax.experimental.pallas import tpu as pltpu
from jax.sharding import PartitionSpec as P

STEPS = 2
BLOCK = 64
HALF = 9
SLOTS = 2 * HALF + 1
LANES = 128
TILES = 10
WIDTH = TILES * LANES
FULL = SLOTS * BLOCK
LINE = 8
EVENS = 9 * BLOCK
ODDS = 10 * BLOCK
MARGIN = 4
STORED = TILES + 9
PARTS = ((0, 3), (4, 6), (7, 9))
MESH = pl.DeviceIdType.MESH

ROUTES = (
    ((1, 1, 0, 1), (7, 0, 0, 7), (8, 0, 1, 0), (-8, 1, -1, 0), (8, 1, 1, 0), (1, 0, 0, 1), (7, 1, 0, 7),
     (-8, 2, -1, 0), (1, 2, 0, 1), (2, 1, 0, 1), (6, 1, 0, 7), (9, 1, 1, 0), (-7, 1, -1, 0), (-1, 1, 0, 7),
     (2, 2, 0, 1), (-1, 0, -1, 0), (9, 0, 1, 0), (-7, 0, -1, 0), (6, 0, 0, 7), (2, 0, 0, 1), (-7, 2, -1, 0),
     (-1, 2, 0, 7), (3, 2, 0, 1), (-6, 1, -1, 0), (-2, 1, 0, 7), (-6, 2, 0, 1), (-9, 1, -1, 0), (4, 2, 0, 2),
     (5, 0, 0, 7), (-2, 0, -1, 0), (-6, 0, -1, 0), (3, 0, 0, 1), (5, 1, 0, 7), (-9, 2, -1, 0), (3, 1, 0, 1),
     (-2, 2, 0, 7), (-5, 2, -1, 0), (-4, 0, -1, 7), (4, 0, 0, 7), (-3, 0, -1, 0), (-4, 2, 0, 2), (-4, 1, 0, 1),
     (-3, 1, -1, 0), (-3, 2, 0, 6), (-5, 0, 0, 1), (4, 1, 0, 7), (-5, 1, -1, 0)),
    ((1, 1, 0, 2), (-1, 0, 0, 0), (-8, 1, -1, 1), (1, 2, 0, 2), (8, 0, 1, 1), (-1, 2, 0, 0), (-8, 2, -1, 1),
     (8, 1, 1, 1), (-1, 1, 0, 0), (1, 0, 0, 2), (9, 1, 1, 1), (-7, 0, -1, 2), (-7, 1, -1, 1), (2, 2, 0, 2),
     (6, 0, 0, 0), (7, 0, 1, 1), (-7, 2, -1, 1), (6, 1, 0, 0), (3, 1, 0, 3), (-9, 2, -1, 1), (7, 1, 1, 1),
     (2, 0, 0, 2), (-9, 1, -1, 1), (5, 1, 0, 0), (2, 1, 0, 2), (9, 0, 1, 1), (-6, 2, -1, 1), (-2, 1, 0, 0),
     (3, 2, 0, 2), (-5, 1, -1, 1), (-2, 0, 0, 0), (-6, 0, -1, 1), (3, 0, 0, 2), (5, 0, 0, 0), (-3, 1, -1, 1),
     (4, 2, 0, 2), (-5, 0, 0, 3), (-2, 2, 0, 0), (-6, 1, -1, 1), (-5, 2, -1, 1), (4, 0, 0, 0), (-4, 0, -1, 2),
     (-4, 1, 0, 2), (4, 1, 0, 0), (-3, 0, -1, 1), (-3, 2, 0, 0), (-4, 2, 0, 2)),
    ((1, 2, 0, 3), (-1, 0, 0, 1), (-8, 1, -1, 2), (1, 0, 0, 3), (-1, 2, 0, 1), (8, 0, 1, 2), (-8, 2, -1, 2),
     (8, 1, 1, 2), (1, 1, 0, 3), (-1, 1, 0, 1), (-7, 2, -1, 2), (-7, 0, -1, 2), (-2, 0, 0, 1), (7, 0, 1, 2),
     (2, 2, 0, 3), (-9, 2, -1, 2), (-2, 2, 0, 1), (-6, 0, -1, 5), (9, 0, 1, 2), (9, 1, 1, 2), (2, 0, 0, 3),
     (-7, 1, -1, 2), (-2, 1, 0, 1), (7, 1, 1, 2), (3, 1, 0, 3), (-9, 1, -1, 2), (3, 2, 0, 3), (5, 0, 0, 1),
     (6, 0, 1, 2), (-6, 2, -1, 2), (5, 1, 0, 1), (6, 1, 1, 2), (3, 0, 0, 3), (2, 1, 0, 1), (-5, 1, -1, 2),
     (4, 2, 0, 3), (-3, 0, -1, 2), (-5, 2, 0, 3), (4, 1, 0, 1), (-5, 0, 0, 3), (-3, 1, -1, 2), (-6, 1, -1, 2),
     (4, 0, 0, 3), (-3, 2, 0, 1), (-4, 0, -1, 1), (-4, 2, 0, 3), (-4, 1, -1, 2)),
    ((-1, 1, 0, 2), (1, 1, 0, 4), (-8, 1, -1, 3), (1, 2, 0, 4), (-1, 0, 0, 2), (8, 0, 1, 3), (-8, 2, -1, 3),
     (8, 1, 1, 3), (-1, 2, 0, 2), (1, 0, 0, 4), (2, 1, 0, 4), (7, 1, 1, 3), (-9, 1, -1, 3), (9, 1, 1, 3),
     (-2, 0, 0, 2), (4, 2, 0, 7), (2, 2, 0, 4), (-7, 1, -1, 3), (-2, 2, 0, 2), (7, 0, 1, 3), (-7, 2, -1, 3),
     (2, 0, 0, 4), (-2, 1, 0, 2), (-7, 0, -1, 3), (9, 0, 1, 3), (3, 2, 0, 4), (-9, 2, -1, 3), (-3, 0, 0, 2),
     (-6, 2, 0, 4), (6, 0, 1, 3), (-6, 1, -1, 3), (-6, 0, -1, 3), (3, 0, 0, 4), (5, 0, 1, 2), (-3, 2, 0, 2),
     (3, 1, 0, 4), (6, 1, 1, 3), (-5, 2, -1, 3), (5, 1, 0, 1), (4, 0, 0, 4), (-3, 1, 0, 2), (-5, 0, 0, 4),
     (-4, 0, -1, 2), (4, 1, 0, 4), (-5, 1, -1, 3), (-4, 1, 0, 1), (-4, 2, 0, 4)),
    ((1, 1, 0, 5), (-1, 0, 0, 3), (-8, 1, -1, 4), (1, 2, 0, 5), (8, 0, 1, 4), (-1, 1, 0, 3), (-8, 2, -1, 4),
     (8, 1, 1, 4), (1, 0, 0, 5), (-1, 2, 0, 3), (9, 1, 1, 4), (2, 2, 0, 5), (-7, 1, -1, 4), (-2, 1, 0, 3),
     (-7, 2, -1, 4), (7, 0, 1, 4), (2, 0, 0, 5), (-2, 0, 0, 3), (7, 1, 1, 4), (-9, 1, -1, 4), (-7, 0, -1, 4),
     (2, 1, 0, 5), (-2, 2, 0, 3), (9, 0, 1, 4), (-9, 2, -1, 4), (6, 1, 1, 4), (-6, 2, -1, 4), (-3, 0, 0, 3),
     (3, 0, 0, 5), (-6, 0, -1, 4), (-3, 2, 0, 3), (3, 1, 0, 5), (-6, 1, -1, 4), (6, 0, 0, 3), (3, 2, 0, 5),
     (-5, 2, -1, 5), (-3, 1, 0, 3), (-5, 0, -1, 4), (-4, 1, 0, 5), (5, 0, 1, 4), (-4, 0, 0, 3), (-5, 1, -1, 4),
     (4, 1, 0, 6), (4, 2, 1, 5), (4, 0, 0, 3), (-4, 2, 0, 3), (5, 1, 1, 4)),
    ((1, 2, 0, 6), (-1, 0, 0, 4), (-8, 1, -1, 5), (1, 0, 0, 6), (8, 0, 1, 5), (-1, 1, 0, 4), (-8, 2, -1, 5),
     (8, 1, 1, 5), (1, 1, 0, 6), (-1, 2, 0, 4), (-7, 2, -1, 5), (-7, 0, -1, 5), (2, 0, 0, 6), (-2, 0, 0, 4),
     (7, 0, 1, 5), (-9, 1, -1, 5), (2, 1, 0, 6), (9, 0, 1, 5), (-7, 1, -1, 5), (2, 2, 0, 6), (-2, 2, 0, 4),
     (7, 1, 1, 5), (9, 1, 1, 5), (-9, 2, -1, 5), (-5, 1, 0, 6), (-3, 1, 0, 4), (-6, 0, -1, 5), (-5, 2, 0, 6),
     (6, 0, 1, 5), (-6, 1, -1, 5), (-5, 0, 0, 6), (-6, 2, -1, 5), (-3, 0, 0, 4), (-4, 1, 0, 6), (3, 1, 1, 5),
     (-3, 2, 0, 4), (-2, 1, 0, 6), (5, 1, 1, 5), (3, 2, 1, 5), (-4, 2, 0, 4), (3, 0, 0, 6), (5, 0, 0, 4),
     (4, 1, 0, 6), (6, 1, 1, 5), (4, 2, 1, 5), (-4, 0, 0, 6), (4, 0, 0, 4)),
    ((1, 0, 0, 7), (-1, 0, 0, 5), (-8, 1, -1, 6), (8, 0, 1, 6), (1, 1, 0, 7), (-1, 1, 0, 5), (-8, 2, -1, 6),
     (8, 1, 1, 6), (1, 2, 0, 7), (-1, 2, 0, 5), (-6, 1, 0, 7), (-2, 0, 0, 5), (9, 0, 1, 6), (-6, 2, 0, 7),
     (-7, 1, -1, 6), (-2, 1, 0, 5), (-6, 0, 0, 7), (7, 0, 1, 6), (-9, 1, -1, 6), (9, 1, 1, 6), (-5, 1, 0, 7),
     (7, 1, 1, 6), (-3, 1, 0, 4), (-7, 2, -1, 6), (-2, 2, 0, 5), (2, 1, 0, 7), (-9, 2, -1, 6), (6, 0, 1, 6),
     (-3, 0, 0, 5), (2, 0, 0, 7), (6, 1, 1, 6), (2, 2, 0, 7), (3, 1, 1, 6), (-4, 0, 0, 4), (-5, 0, 0, 7),
     (-3, 2, 0, 5), (5, 1, 1, 6), (-5, 2, 0, 7), (-7, 0, -1, 4), (-4, 1, 0, 7), (5, 0, 1, 6), (-4, 2, 0, 7),
     (3, 2, 1, 4), (4, 0, 1, 6), (3, 0, 0, 7), (4, 2, 1, 5), (4, 1, 0, 5)),
    ((-1, 1, 0, 6), (-7, 1, 0, 0), (-8, 1, -1, 7), (-7, 2, 0, 0), (8, 0, 1, 7), (-1, 0, 0, 6), (-8, 2, -1, 7),
     (-7, 0, 0, 0), (8, 1, 1, 7), (-1, 2, 0, 6), (-6, 1, 0, 0), (7, 1, 1, 7), (-9, 1, -1, 7), (1, 1, 1, 7),
     (-2, 0, 0, 6), (1, 0, 0, 0), (1, 2, 1, 7), (-6, 0, 0, 0), (-2, 1, 0, 6), (-9, 2, -1, 7), (-6, 2, 0, 0),
     (7, 0, 1, 7), (-2, 2, 0, 6), (9, 1, 1, 7), (-5, 1, 0, 0), (-3, 0, 0, 6), (2, 1, 0, 0), (9, 0, 1, 7),
     (-3, 1, 0, 6), (-5, 2, 0, 0), (6, 1, 1, 7), (6, 0, 0, 6), (2, 2, 1, 7), (2, 0, 0, 0), (-3, 2, 0, 6),
     (3, 1, 1, 7), (-4, 2, 0, 0), (5, 0, 1, 7), (3, 0, 0, 1), (-4, 0, 0, 0), (5, 1, 1, 7), (3, 2, 1, 7),
     (4, 0, 0, 5), (-5, 0, 0, 6), (4, 2, 1, 7), (-4, 1, 0, 0), (4, 1, 0, 6)),
)


def offset_of(d):
    return (d + 1) // 2


def line_of(y, d):
    return (y + d) // LINE


def needed_tiles(d, part):
    first, last = (0, (2 * HALF - d) // 2) if d > 0 else ((-d) // 2, TILES - 1)
    return max(first, PARTS[part][0]), min(last, PARTS[part][1])


def source_slot(y, d, line, column):
    return d + y - line * LINE - column


def receivers(column, slot, part):
    found = []
    for y in range(LINE):
        for d, piece, line, relay in ROUTES[y]:
            if relay == column and piece == part and source_slot(y, d, line, relay) == slot:
                found.append((y, d, -line))
    return found


@functools.cache
def sent_tiles(y, d, part):
    first, last = needed_tiles(d, part)
    for y_next, d_next, _ in receivers(y, d, part):
        first_next, last_next = sent_tiles(y_next, d_next, part)
        first, last = min(first, first_next), max(last, last_next)
    return first, last


@functools.cache
def depth_of(y, d, part):
    return 1 + max([depth_of(y_next, d_next, part) for y_next, d_next, _ in receivers(y, d, part)], default=0)


def sends_from(column):
    own = [(0, part, *entry) for part in range(len(PARTS)) for entry in receivers(column, 0, part)]
    own.sort(key=lambda entry: -depth_of(entry[2], entry[3], entry[1]))
    relayed = [
        (d, part, *entry) for d, part, _, _ in ROUTES[column] for entry in receivers(column, d, part)
    ]
    return own + relayed


MOST_SENDS = max(len(sends_from(column)) for column in range(LINE))


def partners_of(column):
    found = {(line, relay) for _, _, line, relay in ROUTES[column]}
    return sorted(found | {(line, y) for _, _, y, _, line in sends_from(column)})


def kernel(lines, columns, dens_hbm, pat_hbm, out_ref, dens_ref, pat_ref, band, shifted, squares, low, load_sem, send_sem, recv_sem):
    load = pltpu.make_async_copy(dens_hbm, dens_ref, load_sem.at[0])
    load.start()
    load_pattern = pltpu.make_async_copy(pat_hbm, pat_ref, load_sem.at[1])
    load_pattern.start()
    me = lax.axis_index("row") * columns + lax.axis_index("col")
    my_line = me // LINE
    my_column = lax.rem(me, LINE)

    def place(line, y):
        index = (my_line + line) * LINE + y
        return (index // columns, lax.rem(index, columns))

    there = {line: (my_line + line >= 0) & (my_line + line < lines) for line in range(-2, 3)}

    def rows_of(step, d):
        order = (d + HALF - 1) // 2 if d % 2 == 0 else HALF + (d + HALF) // 2
        return pl.ds(pl.multiple_of(step * FULL + order * BLOCK, BLOCK), BLOCK)

    def lanes_of(d, first, last):
        return pl.ds((MARGIN + offset_of(d) + first) * LANES, (last - first + 1) * LANES)

    def copy(step, number, slot, part, y, d, line):
        first, last = sent_tiles(y, d, part)
        return pltpu.make_async_remote_copy(
            src_ref=band.at[rows_of(step, slot), lanes_of(slot, first, last)],
            dst_ref=band.at[rows_of(step, d), lanes_of(d, first, last)],
            send_sem=send_sem.at[step, number],
            recv_sem=recv_sem.at[step, len(PARTS) * (d + HALF) + part],
            device_id=place(line, y),
            device_id_type=MESH,
        )

    def arrival(step, y, d, part):
        first, last = sent_tiles(y, d, part)
        piece = band.at[rows_of(step, d), lanes_of(d, first, last)]
        return pltpu.make_async_remote_copy(
            src_ref=piece,
            dst_ref=piece,
            send_sem=send_sem.at[step, 0],
            recv_sem=recv_sem.at[step, len(PARTS) * (d + HALF) + part],
            device_id=place(0, y),
            device_id_type=MESH,
        )

    def each_column(body):
        for column in range(LINE):
            pl.when(my_column == column)(functools.partial(body, column))

    def sent_when(column, slot, line):
        return there[line] & there[line_of(column, slot)]

    barrier = pltpu.get_barrier_semaphore()

    def greet(column):
        for line, y in partners_of(column):
            @pl.when(there[line])
            def _():
                pl.semaphore_signal(barrier, inc=1, device_id=place(line, y), device_id_type=MESH)

    def meet(column):
        count = jnp.int32(0)
        for line, _ in partners_of(column):
            count += there[line].astype(jnp.int32)
        pl.semaphore_wait(barrier, count)

    each_column(greet)
    load.wait()
    padded = jnp.concatenate([dens_ref[...], jnp.zeros((BLOCK, WIDTH - FULL), jnp.float32)], axis=1)
    band[rows_of(0, 0), MARGIN * LANES:(MARGIN + TILES) * LANES] = padded.astype(jnp.bfloat16)
    each_column(meet)
    load_pattern.wait()

    def clear():
        for step in range(STEPS):
            for d in range(-HALF, HALF + 1):
                off = offset_of(d)
                if d > 0:
                    band[rows_of(step, d), MARGIN * LANES:(MARGIN + off) * LANES] = jnp.zeros(
                        (BLOCK, off * LANES), jnp.bfloat16
                    )
                elif off < 0:
                    band[rows_of(step, d), (MARGIN + TILES + off) * LANES:(MARGIN + TILES) * LANES] = jnp.zeros(
                        (BLOCK, -off * LANES), jnp.bfloat16
                    )
                if d != 0:
                    @pl.when((me + d < 0) | (me + d >= lines * LINE))
                    def _():
                        band[rows_of(step, d), MARGIN * LANES:(MARGIN + TILES) * LANES] = jnp.zeros(
                            (BLOCK, WIDTH), jnp.bfloat16
                        )
        low[0:BLOCK, :] = jnp.zeros((BLOCK, BLOCK), jnp.bfloat16)
        low[(SLOTS + 1) * BLOCK:(SLOTS + 2) * BLOCK, :] = jnp.zeros((BLOCK, BLOCK), jnp.bfloat16)
        squares[(SLOTS + 1) * BLOCK:(SLOTS + 2) * BLOCK, :] = jnp.zeros((BLOCK, BLOCK), jnp.float32)
        squares[0:BLOCK, :] = jnp.zeros((BLOCK, BLOCK), jnp.float32)

    window = pl.ds(MARGIN * LANES, WIDTH)

    def purify(step, _):
        def offer(column):
            for number, entry in enumerate(sends_from(column)):
                if entry[0] == 0:
                    @pl.when(sent_when(column, 0, entry[4]))
                    def _():
                        copy(step, number, *entry).start()

        def relay(column):
            sends = sends_from(column)
            for d, part, _, _ in ROUTES[column]:
                @pl.when(there[line_of(column, d)])
                def _():
                    arrival(step, column, d, part).wait_recv()

                for number, entry in enumerate(sends):
                    if entry[:2] == (d, part):
                        @pl.when(sent_when(column, d, entry[4]))
                        def _():
                            copy(step, number, *entry).start()

        each_column(offer)

        @pl.when(step == 0)
        def _():
            clear()
            padded = jnp.concatenate([jnp.zeros((BLOCK, BLOCK), jnp.float32), dens_ref[...]], axis=1)
            shifted[...] = padded.astype(jnp.bfloat16)

        @pl.when(step > 0)
        def _():
            for tile in range(TILES):
                part = squares[2 * tile * BLOCK:(2 + 2 * tile) * BLOCK, :]
                shifted[:, tile * LANES:(1 + tile) * LANES] = part.T.astype(jnp.bfloat16)

        each_column(relay)
        own = band[rows_of(step, 0), window]
        even_rows = band[pl.ds(pl.multiple_of(step * FULL, BLOCK), EVENS), window]
        odd_rows = band[pl.ds(pl.multiple_of(step * FULL + EVENS, BLOCK), ODDS), window]
        across = (((1,), (1,)), ((), ()))
        even_square = lax.dot_general(even_rows, own, across, preferred_element_type=jnp.float32)
        odd_square = lax.dot_general(odd_rows, shifted[...], across, preferred_element_type=jnp.float32)
        for slot in range(SLOTS):
            order = (slot - 1) // 2 if slot % 2 else slot // 2
            source = even_square if slot % 2 else odd_square
            kept = pat_ref[0, slot].astype(jnp.float32)
            part = source[order * BLOCK:(order + 1) * BLOCK, :] * kept
            squares[(1 + slot) * BLOCK:(2 + slot) * BLOCK, :] = part
            low[(1 + slot) * BLOCK:(2 + slot) * BLOCK, :] = part.astype(jnp.bfloat16)
        even_cube = jnp.dot(even_rows, low[BLOCK:BLOCK + WIDTH, :], preferred_element_type=jnp.float32)
        odd_cube = jnp.dot(odd_rows, low[0:WIDTH, :], preferred_element_type=jnp.float32)
        for slot in range(SLOTS):
            order = (slot - 1) // 2 if slot % 2 else slot // 2
            source = even_cube if slot % 2 else odd_cube
            kept = pat_ref[0, slot].astype(jnp.float32)
            part = squares[(1 + slot) * BLOCK:(2 + slot) * BLOCK, :]
            cube = source[order * BLOCK:(order + 1) * BLOCK, :]
            squares[(1 + slot) * BLOCK:(2 + slot) * BLOCK, :] = (3.0 * part - 2.0 * cube) * kept

        @pl.when(step < STEPS - 1)
        def _():
            for tile in range(TILES):
                part = squares[(1 + 2 * tile) * BLOCK:(3 + 2 * tile) * BLOCK, :]
                band[rows_of(step + 1, 0), (MARGIN + tile) * LANES:(MARGIN + 1 + tile) * LANES] = part.T.astype(
                    jnp.bfloat16
                )

        return 0

    lax.fori_loop(0, STEPS, purify, 0)

    for tile in range(TILES):
        part = squares[(1 + 2 * tile) * BLOCK:(3 + 2 * tile) * BLOCK, :].T
        wide = min(LANES, FULL - tile * LANES)
        out_ref[:, tile * LANES:tile * LANES + wide] = part[:, :wide]

    def finish(step, _):
        def drain(column):
            for number, entry in enumerate(sends_from(column)):
                @pl.when(sent_when(column, entry[0], entry[4]))
                def _():
                    copy(step, number, *entry).wait_send()

        each_column(drain)
        return 0

    lax.fori_loop(0, STEPS, finish, 0)


def solution(mesh):
    columns = mesh.shape["col"]
    lines = mesh.shape["row"] * columns // LINE

    def local(density, pattern):
        return pl.pallas_call(
            functools.partial(kernel, lines, columns),
            out_shape=jax.ShapeDtypeStruct((BLOCK, FULL), jnp.float32),
            in_specs=[
                pl.BlockSpec(memory_space=pltpu.HBM),
                pl.BlockSpec(memory_space=pltpu.HBM),
            ],
            out_specs=pl.BlockSpec(memory_space=pltpu.VMEM),
            scratch_shapes=[
                pltpu.VMEM((BLOCK, FULL), jnp.float32),
                pltpu.SMEM((1, SLOTS), jnp.int32),
                pltpu.VMEM((STEPS * FULL, STORED * LANES), jnp.bfloat16),
                pltpu.VMEM((BLOCK, WIDTH), jnp.bfloat16),
                pltpu.VMEM(((SLOTS + 2) * BLOCK, BLOCK), jnp.float32),
                pltpu.VMEM(((SLOTS + 2) * BLOCK, BLOCK), jnp.bfloat16),
                pltpu.SemaphoreType.DMA((2,)),
                pltpu.SemaphoreType.DMA((STEPS, MOST_SENDS)),
                pltpu.SemaphoreType.DMA((STEPS, len(PARTS) * SLOTS)),
            ],
            compiler_params=pltpu.CompilerParams(
                collective_id=0, has_side_effects=True, vmem_limit_bytes=40 << 20
            ),
        )(density, pattern)

    placed = (P(("row", "col"), None), P(("row", "col"), None))
    return jax.shard_map(
        local, mesh=mesh, in_specs=placed, out_specs=P(("row", "col"), None), check_vma=False
    )
```

time: 67.6 us -> 62.7 us (0.928)
  Pallas kernels: 65.1 us -> 60.2 us
    pallas_call x1, Pallas kernels: 65.1 us -> 60.2 us  [local(): pl.pallas_call(functools.partial(kernel, lines, columns), out_shape=jax.S...]
where the time goes in v3:
time: 62.7 us; the launch traced here: 62.6 us
  Pallas kernels  60.2 us (96%)
  local copies, waits for them, and re-layouts  2.35 us (4%)
    pallas_call x1, Pallas kernels, local(): pl.pallas_call(functools.partial(kernel, lines, columns), out_shape=jax.S...  60.2 us
    unnamed x5, local copies, waits for them, and re-layouts  2.35 us

profile of v3, /device:TPU:1, one launch (start us, length us, event | category | flops | bytes accessed | tf_op | source)
XLA Modules:
  0.0 62.6 jit_solution(16538756727305958179)
XLA Ops:
  0.0 0.0 copy-start
  0.0 1.0 %copy-done = f32[64,1216]{1,0:T(8,128)S(1)} copy-done((f32[64,1216]{1,0:T(8,128)S(1)}, f32[64,1216]{1,0:T(8,128)}, u32[]{:S(2)}) %copy-start) | copy-done | bytes 311320
  1.0 0.0 copy-start.1
  1.0 0.7 %copy-done.1 = s32[1,19]{1,0:T(1,128)S(1)} copy-done((s32[1,19]{1,0:T(1,128)S(1)}, s32[1,19]{1,0:T(1,128)}, u32[]{:S(2)}) %copy-start.1) | copy-done | bytes 100
  1.6 60.2 %shard_map.28 = f32[64,1216]{1,0:T(8,128)S(1)} custom-call(f32[64,1216]{1,0:T(8,128)S(1)} %copy-done, s32[1,19]{1,0:T(1,128)S(1)} %copy-done.1), custom_call_target="tpu_custom_call" | custom-call | tf_op jit(solution)/shard_map/pallas_call | solution.py:335
  61.8 0.7 %copy.4 = f32[64,1216]{1,0:T(8,128)} copy(f32[64,1216]{1,0:T(8,128)S(1)} %shard_map.28) | data formatting | bytes 622592
Async XLA Ops:
  0.0 1.0 %copy-start = (f32[64,1216]{1,0:T(8,128)S(1)}, f32[64,1216]{1,0:T(8,128)}, u32[]{:S(2)}) copy-start(f32[64,1216]{1,0:T(8,128)} %dens_hbm.1) | copy-start | bytes 933892
  1.0 0.7 %copy-start.1 = (s32[1,19]{1,0:T(1,128)S(1)}, s32[1,19]{1,0:T(1,128)}, u32[]{:S(2)}) copy-start(s32[1,19]{1,0:T(1,128)} %pat_hbm.1) | copy-start | bytes 232

commit v4 on v3

--- a/solution.py
+++ b/solution.py
@@ -20,66 +20,99 @@
 ODDS = 10 * BLOCK
 MARGIN = 4
 STORED = TILES + 9
-PARTS = ((0, 3), (4, 6), (7, 9))
+PARTS = ((0, 1), (2, 3), (4, 5), (6, 7), (8, 9))
+DELAY = 20
 MESH = pl.DeviceIdType.MESH
 
 ROUTES = (
-    ((1, 1, 0, 1), (7, 0, 0, 7), (8, 0, 1, 0), (-8, 1, -1, 0), (8, 1, 1, 0), (1, 0, 0, 1), (7, 1, 0, 7),
-     (-8, 2, -1, 0), (1, 2, 0, 1), (2, 1, 0, 1), (6, 1, 0, 7), (9, 1, 1, 0), (-7, 1, -1, 0), (-1, 1, 0, 7),
-     (2, 2, 0, 1), (-1, 0, -1, 0), (9, 0, 1, 0), (-7, 0, -1, 0), (6, 0, 0, 7), (2, 0, 0, 1), (-7, 2, -1, 0),
-     (-1, 2, 0, 7), (3, 2, 0, 1), (-6, 1, -1, 0), (-2, 1, 0, 7), (-6, 2, 0, 1), (-9, 1, -1, 0), (4, 2, 0, 2),
-     (5, 0, 0, 7), (-2, 0, -1, 0), (-6, 0, -1, 0), (3, 0, 0, 1), (5, 1, 0, 7), (-9, 2, -1, 0), (3, 1, 0, 1),
-     (-2, 2, 0, 7), (-5, 2, -1, 0), (-4, 0, -1, 7), (4, 0, 0, 7), (-3, 0, -1, 0), (-4, 2, 0, 2), (-4, 1, 0, 1),
-     (-3, 1, -1, 0), (-3, 2, 0, 6), (-5, 0, 0, 1), (4, 1, 0, 7), (-5, 1, -1, 0)),
-    ((1, 1, 0, 2), (-1, 0, 0, 0), (-8, 1, -1, 1), (1, 2, 0, 2), (8, 0, 1, 1), (-1, 2, 0, 0), (-8, 2, -1, 1),
-     (8, 1, 1, 1), (-1, 1, 0, 0), (1, 0, 0, 2), (9, 1, 1, 1), (-7, 0, -1, 2), (-7, 1, -1, 1), (2, 2, 0, 2),
-     (6, 0, 0, 0), (7, 0, 1, 1), (-7, 2, -1, 1), (6, 1, 0, 0), (3, 1, 0, 3), (-9, 2, -1, 1), (7, 1, 1, 1),
-     (2, 0, 0, 2), (-9, 1, -1, 1), (5, 1, 0, 0), (2, 1, 0, 2), (9, 0, 1, 1), (-6, 2, -1, 1), (-2, 1, 0, 0),
-     (3, 2, 0, 2), (-5, 1, -1, 1), (-2, 0, 0, 0), (-6, 0, -1, 1), (3, 0, 0, 2), (5, 0, 0, 0), (-3, 1, -1, 1),
-     (4, 2, 0, 2), (-5, 0, 0, 3), (-2, 2, 0, 0), (-6, 1, -1, 1), (-5, 2, -1, 1), (4, 0, 0, 0), (-4, 0, -1, 2),
-     (-4, 1, 0, 2), (4, 1, 0, 0), (-3, 0, -1, 1), (-3, 2, 0, 0), (-4, 2, 0, 2)),
-    ((1, 2, 0, 3), (-1, 0, 0, 1), (-8, 1, -1, 2), (1, 0, 0, 3), (-1, 2, 0, 1), (8, 0, 1, 2), (-8, 2, -1, 2),
-     (8, 1, 1, 2), (1, 1, 0, 3), (-1, 1, 0, 1), (-7, 2, -1, 2), (-7, 0, -1, 2), (-2, 0, 0, 1), (7, 0, 1, 2),
-     (2, 2, 0, 3), (-9, 2, -1, 2), (-2, 2, 0, 1), (-6, 0, -1, 5), (9, 0, 1, 2), (9, 1, 1, 2), (2, 0, 0, 3),
-     (-7, 1, -1, 2), (-2, 1, 0, 1), (7, 1, 1, 2), (3, 1, 0, 3), (-9, 1, -1, 2), (3, 2, 0, 3), (5, 0, 0, 1),
-     (6, 0, 1, 2), (-6, 2, -1, 2), (5, 1, 0, 1), (6, 1, 1, 2), (3, 0, 0, 3), (2, 1, 0, 1), (-5, 1, -1, 2),
-     (4, 2, 0, 3), (-3, 0, -1, 2), (-5, 2, 0, 3), (4, 1, 0, 1), (-5, 0, 0, 3), (-3, 1, -1, 2), (-6, 1, -1, 2),
-     (4, 0, 0, 3), (-3, 2, 0, 1), (-4, 0, -1, 1), (-4, 2, 0, 3), (-4, 1, -1, 2)),
-    ((-1, 1, 0, 2), (1, 1, 0, 4), (-8, 1, -1, 3), (1, 2, 0, 4), (-1, 0, 0, 2), (8, 0, 1, 3), (-8, 2, -1, 3),
-     (8, 1, 1, 3), (-1, 2, 0, 2), (1, 0, 0, 4), (2, 1, 0, 4), (7, 1, 1, 3), (-9, 1, -1, 3), (9, 1, 1, 3),
-     (-2, 0, 0, 2), (4, 2, 0, 7), (2, 2, 0, 4), (-7, 1, -1, 3), (-2, 2, 0, 2), (7, 0, 1, 3), (-7, 2, -1, 3),
-     (2, 0, 0, 4), (-2, 1, 0, 2), (-7, 0, -1, 3), (9, 0, 1, 3), (3, 2, 0, 4), (-9, 2, -1, 3), (-3, 0, 0, 2),
-     (-6, 2, 0, 4), (6, 0, 1, 3), (-6, 1, -1, 3), (-6, 0, -1, 3), (3, 0, 0, 4), (5, 0, 1, 2), (-3, 2, 0, 2),
-     (3, 1, 0, 4), (6, 1, 1, 3), (-5, 2, -1, 3), (5, 1, 0, 1), (4, 0, 0, 4), (-3, 1, 0, 2), (-5, 0, 0, 4),
-     (-4, 0, -1, 2), (4, 1, 0, 4), (-5, 1, -1, 3), (-4, 1, 0, 1), (-4, 2, 0, 4)),
-    ((1, 1, 0, 5), (-1, 0, 0, 3), (-8, 1, -1, 4), (1, 2, 0, 5), (8, 0, 1, 4), (-1, 1, 0, 3), (-8, 2, -1, 4),
-     (8, 1, 1, 4), (1, 0, 0, 5), (-1, 2, 0, 3), (9, 1, 1, 4), (2, 2, 0, 5), (-7, 1, -1, 4), (-2, 1, 0, 3),
-     (-7, 2, -1, 4), (7, 0, 1, 4), (2, 0, 0, 5), (-2, 0, 0, 3), (7, 1, 1, 4), (-9, 1, -1, 4), (-7, 0, -1, 4),
-     (2, 1, 0, 5), (-2, 2, 0, 3), (9, 0, 1, 4), (-9, 2, -1, 4), (6, 1, 1, 4), (-6, 2, -1, 4), (-3, 0, 0, 3),
-     (3, 0, 0, 5), (-6, 0, -1, 4), (-3, 2, 0, 3), (3, 1, 0, 5), (-6, 1, -1, 4), (6, 0, 0, 3), (3, 2, 0, 5),
-     (-5, 2, -1, 5), (-3, 1, 0, 3), (-5, 0, -1, 4), (-4, 1, 0, 5), (5, 0, 1, 4), (-4, 0, 0, 3), (-5, 1, -1, 4),
-     (4, 1, 0, 6), (4, 2, 1, 5), (4, 0, 0, 3), (-4, 2, 0, 3), (5, 1, 1, 4)),
-    ((1, 2, 0, 6), (-1, 0, 0, 4), (-8, 1, -1, 5), (1, 0, 0, 6), (8, 0, 1, 5), (-1, 1, 0, 4), (-8, 2, -1, 5),
-     (8, 1, 1, 5), (1, 1, 0, 6), (-1, 2, 0, 4), (-7, 2, -1, 5), (-7, 0, -1, 5), (2, 0, 0, 6), (-2, 0, 0, 4),
-     (7, 0, 1, 5), (-9, 1, -1, 5), (2, 1, 0, 6), (9, 0, 1, 5), (-7, 1, -1, 5), (2, 2, 0, 6), (-2, 2, 0, 4),
-     (7, 1, 1, 5), (9, 1, 1, 5), (-9, 2, -1, 5), (-5, 1, 0, 6), (-3, 1, 0, 4), (-6, 0, -1, 5), (-5, 2, 0, 6),
-     (6, 0, 1, 5), (-6, 1, -1, 5), (-5, 0, 0, 6), (-6, 2, -1, 5), (-3, 0, 0, 4), (-4, 1, 0, 6), (3, 1, 1, 5),
-     (-3, 2, 0, 4), (-2, 1, 0, 6), (5, 1, 1, 5), (3, 2, 1, 5), (-4, 2, 0, 4), (3, 0, 0, 6), (5, 0, 0, 4),
-     (4, 1, 0, 6), (6, 1, 1, 5), (4, 2, 1, 5), (-4, 0, 0, 6), (4, 0, 0, 4)),
-    ((1, 0, 0, 7), (-1, 0, 0, 5), (-8, 1, -1, 6), (8, 0, 1, 6), (1, 1, 0, 7), (-1, 1, 0, 5), (-8, 2, -1, 6),
-     (8, 1, 1, 6), (1, 2, 0, 7), (-1, 2, 0, 5), (-6, 1, 0, 7), (-2, 0, 0, 5), (9, 0, 1, 6), (-6, 2, 0, 7),
-     (-7, 1, -1, 6), (-2, 1, 0, 5), (-6, 0, 0, 7), (7, 0, 1, 6), (-9, 1, -1, 6), (9, 1, 1, 6), (-5, 1, 0, 7),
-     (7, 1, 1, 6), (-3, 1, 0, 4), (-7, 2, -1, 6), (-2, 2, 0, 5), (2, 1, 0, 7), (-9, 2, -1, 6), (6, 0, 1, 6),
-     (-3, 0, 0, 5), (2, 0, 0, 7), (6, 1, 1, 6), (2, 2, 0, 7), (3, 1, 1, 6), (-4, 0, 0, 4), (-5, 0, 0, 7),
-     (-3, 2, 0, 5), (5, 1, 1, 6), (-5, 2, 0, 7), (-7, 0, -1, 4), (-4, 1, 0, 7), (5, 0, 1, 6), (-4, 2, 0, 7),
-     (3, 2, 1, 4), (4, 0, 1, 6), (3, 0, 0, 7), (4, 2, 1, 5), (4, 1, 0, 5)),
-    ((-1, 1, 0, 6), (-7, 1, 0, 0), (-8, 1, -1, 7), (-7, 2, 0, 0), (8, 0, 1, 7), (-1, 0, 0, 6), (-8, 2, -1, 7),
-     (-7, 0, 0, 0), (8, 1, 1, 7), (-1, 2, 0, 6), (-6, 1, 0, 0), (7, 1, 1, 7), (-9, 1, -1, 7), (1, 1, 1, 7),
-     (-2, 0, 0, 6), (1, 0, 0, 0), (1, 2, 1, 7), (-6, 0, 0, 0), (-2, 1, 0, 6), (-9, 2, -1, 7), (-6, 2, 0, 0),
-     (7, 0, 1, 7), (-2, 2, 0, 6), (9, 1, 1, 7), (-5, 1, 0, 0), (-3, 0, 0, 6), (2, 1, 0, 0), (9, 0, 1, 7),
-     (-3, 1, 0, 6), (-5, 2, 0, 0), (6, 1, 1, 7), (6, 0, 0, 6), (2, 2, 1, 7), (2, 0, 0, 0), (-3, 2, 0, 6),
-     (3, 1, 1, 7), (-4, 2, 0, 0), (5, 0, 1, 7), (3, 0, 0, 1), (-4, 0, 0, 0), (5, 1, 1, 7), (3, 2, 1, 7),
-     (4, 0, 0, 5), (-5, 0, 0, 6), (4, 2, 1, 7), (-4, 1, 0, 0), (4, 1, 0, 6)),
+    ((1, 3, 0, 1), (7, 0, 0, 7), (8, 0, 1, 0), (1, 0, 0, 1), (7, 1, 0, 7), (8, 1, 1, 0), (1, 1, 0, 1),
+     (7, 2, 0, 7), (-8, 3, -1, 0), (8, 2, 1, 0), (1, 2, 0, 1), (-8, 2, -1, 0), (1, 4, 0, 1), (-8, 4, -1, 0),
+     (-1, 4, 0, 7), (2, 1, 0, 1), (-7, 3, -1, 0), (6, 1, 0, 7), (9, 0, 1, 0), (2, 2, 0, 1), (-1, 0, -1, 0),
+     (6, 0, 0, 7), (9, 1, 1, 0), (2, 3, 0, 1), (-1, 1, -1, 0), (-1, 3, 0, 7), (-7, 1, -1, 0), (9, 2, 1, 0),
+     (2, 4, 0, 1), (6, 2, 0, 7), (-7, 2, -1, 0), (2, 0, 0, 1), (-1, 2, 0, 7), (-7, 4, -1, 0), (3, 1, 0, 1),
+     (6, 3, 0, 7), (-9, 4, -1, 0), (5, 2, 0, 7), (-6, 1, -1, 0), (-6, 2, 0, 1), (5, 3, 0, 7), (-2, 1, -1, 0),
+     (-2, 0, -1, 0), (-2, 2, 0, 7), (3, 0, 0, 1), (-6, 3, -1, 0), (5, 0, 0, 7), (4, 1, 0, 1), (-9, 3, -1, 0),
+     (5, 1, 0, 7), (-5, 1, 0, 1), (-6, 4, -1, 0), (-2, 3, 0, 7), (4, 2, 0, 1), (-9, 2, -1, 0), (-2, 4, 0, 7),
+     (-5, 3, 0, 1), (-3, 2, -1, 0), (4, 3, 0, 7), (-5, 2, 0, 1), (-3, 3, -1, 0), (4, 0, 0, 7), (-3, 0, -1, 0),
+     (3, 2, 0, 7), (-4, 1, -1, 0), (-4, 4, 0, 2), (-5, 4, 0, 1), (3, 3, 0, 7), (-3, 1, -1, 0), (-3, 4, 0, 2),
+     (-4, 2, 0, 1), (-4, 3, -1, 0)),
+    ((-1, 2, 0, 0), (1, 1, 0, 2), (-1, 0, 0, 0), (1, 2, 0, 2), (-1, 1, 0, 0), (1, 3, 0, 2), (-8, 2, -1, 1),
+     (8, 0, 1, 1), (-1, 3, 0, 0), (1, 4, 0, 2), (-8, 3, -1, 1), (8, 1, 1, 1), (-1, 4, 0, 0), (1, 0, 0, 2),
+     (-8, 4, -1, 1), (8, 2, 1, 1), (2, 1, 0, 2), (-9, 2, -1, 1), (6, 3, 0, 7), (6, 0, 0, 0), (-7, 1, -1, 1),
+     (7, 2, 1, 1), (2, 2, 0, 2), (6, 1, 0, 0), (-7, 2, -1, 1), (9, 1, 1, 1), (2, 3, 0, 2), (6, 2, 0, 0),
+     (-7, 3, -1, 1), (7, 0, 1, 1), (2, 4, 0, 2), (9, 2, 1, 1), (-9, 3, 0, 0), (-7, 4, -1, 1), (2, 0, 0, 2),
+     (7, 1, 1, 1), (-2, 4, 0, 0), (-9, 4, -1, 1), (3, 1, 0, 2), (9, 0, 1, 1), (5, 1, 0, 0), (-6, 1, -1, 1),
+     (3, 2, 0, 2), (-2, 0, -1, 1), (5, 0, 0, 0), (-6, 3, 0, 2), (-6, 2, -1, 1), (-2, 3, 0, 0), (3, 3, 0, 2),
+     (-2, 1, -1, 1), (5, 2, 0, 0), (3, 0, 0, 2), (-2, 2, -1, 1), (-6, 4, -1, 1), (4, 1, 0, 2), (4, 2, 0, 0),
+     (-5, 1, -1, 1), (4, 3, 0, 0), (-5, 2, 0, 2), (-3, 1, -1, 1), (-3, 0, 0, 0), (-5, 3, -1, 1), (-3, 2, 0, 0),
+     (4, 0, 0, 0), (-5, 4, 0, 2), (5, 3, 0, 2), (-4, 1, -1, 0), (-4, 2, -1, 1), (-3, 3, 0, 0), (-4, 3, -1, 1),
+     (-3, 4, 0, 0), (-4, 4, 0, 2)),
+    ((1, 1, 0, 3), (-1, 0, 0, 1), (1, 2, 0, 3), (-1, 1, 0, 1), (1, 3, 0, 3), (-8, 2, -1, 2), (-1, 2, 0, 1),
+     (8, 0, 1, 2), (1, 4, 0, 3), (-8, 3, -1, 2), (-1, 3, 0, 1), (8, 1, 1, 2), (1, 0, 0, 3), (-8, 4, -1, 2),
+     (-1, 4, 0, 1), (-7, 1, -1, 2), (8, 2, 1, 2), (2, 1, 0, 3), (-2, 2, 0, 1), (9, 1, 1, 2), (-7, 2, -1, 2),
+     (2, 2, 0, 3), (-2, 0, 0, 1), (7, 0, 1, 2), (-7, 3, -1, 2), (2, 3, 0, 3), (9, 2, 1, 2), (-2, 1, 0, 1),
+     (-9, 2, -1, 2), (2, 4, 0, 3), (7, 1, 1, 2), (-2, 3, 0, 1), (-7, 4, -1, 2), (2, 0, 0, 3), (7, 2, 1, 2),
+     (-2, 4, 0, 1), (5, 3, 0, 1), (-9, 3, -1, 2), (9, 0, 1, 2), (3, 1, 0, 3), (5, 0, 0, 1), (-9, 4, -1, 2),
+     (6, 2, 1, 2), (-6, 1, -1, 2), (3, 2, 0, 3), (5, 1, 0, 1), (6, 0, 1, 2), (-6, 2, -1, 2), (3, 3, 0, 3),
+     (5, 2, 0, 1), (6, 1, 1, 2), (-6, 3, -1, 2), (3, 0, 0, 3), (6, 3, 1, 2), (-3, 4, 0, 1), (-6, 4, -1, 2),
+     (4, 2, 0, 3), (4, 1, 0, 1), (-5, 1, -1, 2), (-3, 0, 0, 1), (4, 3, 0, 3), (-5, 2, -1, 2), (-5, 4, 0, 3),
+     (4, 0, 0, 1), (-3, 1, -1, 2), (-3, 3, 0, 1), (-5, 3, -1, 2), (-3, 2, -1, 2), (-4, 4, 0, 3), (-4, 2, -1, 2),
+     (-4, 1, -1, 2), (-4, 3, -1, 2)),
+    ((1, 1, 0, 4), (-1, 0, 0, 2), (1, 2, 0, 4), (-1, 1, 0, 2), (1, 3, 0, 4), (-8, 2, -1, 3), (-1, 2, 0, 2),
+     (8, 0, 1, 3), (1, 4, 0, 4), (-8, 3, -1, 3), (-1, 3, 0, 2), (8, 1, 1, 3), (1, 0, 0, 4), (-8, 4, -1, 3),
+     (-1, 4, 0, 2), (-7, 1, -1, 3), (8, 2, 1, 3), (2, 4, 0, 4), (-2, 0, 0, 2), (9, 1, 1, 3), (-7, 2, -1, 3),
+     (2, 1, 0, 4), (-2, 1, 0, 2), (7, 0, 1, 3), (-7, 3, -1, 3), (2, 2, 0, 4), (9, 2, 1, 3), (-2, 2, 0, 2),
+     (-9, 2, -1, 3), (2, 3, 0, 4), (7, 1, 1, 3), (-2, 3, 0, 2), (-7, 4, -1, 3), (2, 0, 0, 4), (7, 2, 1, 3),
+     (-2, 4, 0, 2), (-9, 3, -1, 3), (3, 2, 0, 4), (9, 0, 1, 3), (-3, 2, 0, 2), (-9, 4, -1, 3), (3, 3, 0, 4),
+     (6, 0, 1, 3), (-3, 0, 0, 2), (-6, 4, -1, 3), (3, 1, 0, 4), (6, 1, 1, 3), (-6, 1, -1, 3), (-3, 1, 0, 2),
+     (6, 2, 1, 3), (-6, 2, -1, 3), (-3, 3, 0, 2), (6, 3, 1, 3), (3, 0, 0, 4), (-5, 4, -1, 4), (5, 2, 1, 3),
+     (-6, 3, -1, 3), (4, 0, 0, 2), (4, 1, 0, 4), (-5, 2, -1, 3), (5, 0, 0, 2), (5, 1, 1, 3), (5, 3, 1, 3),
+     (4, 2, 0, 2), (-4, 1, -1, 4), (-5, 3, -1, 3), (-4, 4, 0, 2), (4, 3, 0, 4), (-3, 4, 0, 4), (-4, 2, -1, 4),
+     (-5, 1, -1, 3), (-4, 3, -1, 4)),
+    ((1, 4, 0, 5), (-1, 2, 0, 3), (1, 1, 0, 5), (-1, 3, 0, 3), (1, 2, 0, 5), (-8, 2, -1, 4), (-1, 0, 0, 3),
+     (8, 0, 1, 4), (1, 3, 0, 5), (-8, 3, -1, 4), (-1, 1, 0, 3), (8, 1, 1, 4), (1, 0, 0, 5), (-8, 4, -1, 4),
+     (-1, 4, 0, 3), (8, 2, 1, 4), (2, 2, 0, 5), (-7, 4, -1, 4), (-2, 0, 0, 3), (7, 2, 1, 4), (2, 3, 0, 5),
+     (-9, 2, -1, 4), (-2, 1, 0, 3), (-7, 1, -1, 4), (9, 1, 1, 4), (2, 1, 0, 5), (9, 2, 1, 4), (-2, 2, 0, 3),
+     (-9, 3, -1, 4), (2, 4, 0, 5), (7, 0, 1, 4), (-2, 3, 0, 3), (-7, 2, -1, 4), (2, 0, 0, 5), (7, 1, 1, 4),
+     (-2, 4, 0, 3), (-7, 3, -1, 4), (9, 0, 1, 4), (-3, 0, 0, 3), (3, 1, 0, 5), (-9, 4, -1, 4), (6, 0, 1, 4),
+     (-3, 1, 0, 3), (3, 2, 0, 5), (-6, 2, -1, 4), (6, 1, 1, 4), (-3, 2, 0, 3), (3, 3, 0, 5), (-6, 3, -1, 4),
+     (-6, 1, -1, 4), (6, 2, 1, 4), (-3, 3, 0, 3), (3, 0, 0, 5), (6, 3, 1, 4), (-6, 4, -1, 4), (-3, 4, 0, 3),
+     (5, 0, 1, 4), (-4, 4, 0, 5), (-5, 4, -1, 5), (-5, 1, -1, 4), (-4, 2, 0, 5), (4, 2, 1, 3), (5, 1, 1, 4),
+     (-5, 2, -1, 4), (-4, 1, 0, 3), (-5, 3, -1, 4), (4, 0, 1, 3), (5, 2, 1, 4), (-4, 3, 0, 3), (5, 3, 1, 4),
+     (4, 1, 1, 3), (4, 3, 1, 3)),
+    ((1, 2, 0, 6), (-1, 3, 0, 4), (1, 3, 0, 6), (-1, 0, 0, 4), (1, 1, 0, 6), (-8, 2, -1, 5), (-1, 1, 0, 4),
+     (8, 0, 1, 5), (1, 4, 0, 6), (-8, 3, -1, 5), (-1, 2, 0, 4), (8, 1, 1, 5), (1, 0, 0, 6), (-8, 4, -1, 5),
+     (-1, 4, 0, 4), (8, 2, 1, 5), (-7, 2, -1, 5), (9, 2, 1, 5), (-2, 2, 0, 4), (2, 1, 0, 6), (-9, 3, -1, 5),
+     (7, 0, 1, 5), (-2, 3, 0, 4), (2, 2, 0, 6), (-7, 3, -1, 5), (9, 1, 1, 5), (-2, 0, 0, 4), (2, 3, 0, 6),
+     (-7, 1, -1, 5), (7, 1, 1, 5), (-2, 1, 0, 4), (2, 0, 0, 6), (-7, 4, -1, 5), (7, 2, 1, 5), (-2, 4, 0, 4),
+     (2, 4, 0, 6), (-9, 2, -1, 5), (9, 0, 1, 5), (-3, 0, 0, 4), (-5, 4, 0, 6), (-9, 4, -1, 5), (-6, 1, -1, 5),
+     (6, 2, 1, 5), (-3, 1, 0, 4), (-5, 2, 0, 6), (6, 3, 1, 5), (-6, 2, -1, 5), (-3, 2, 0, 4), (-5, 3, 0, 6),
+     (6, 0, 1, 5), (-6, 3, -1, 5), (-3, 3, 0, 4), (6, 1, 1, 5), (-3, 4, 0, 4), (-6, 4, -1, 5), (-5, 1, 0, 6),
+     (5, 0, 1, 5), (-4, 3, 0, 6), (-4, 1, 0, 4), (5, 1, 1, 5), (3, 0, 0, 6), (-4, 2, 0, 4), (5, 2, 1, 5),
+     (3, 1, 0, 6), (3, 3, 1, 5), (5, 3, 1, 5), (-4, 4, 0, 6), (4, 0, 0, 4), (4, 3, 1, 5), (4, 1, 1, 5),
+     (3, 2, 0, 4), (4, 2, 1, 5)),
+    ((-1, 2, 0, 5), (1, 1, 0, 7), (-1, 3, 0, 5), (1, 2, 0, 7), (-8, 2, -1, 6), (-1, 0, 0, 5), (8, 0, 1, 6),
+     (1, 3, 0, 7), (-8, 3, -1, 6), (-1, 1, 0, 5), (8, 1, 1, 6), (1, 0, 0, 7), (-8, 4, -1, 6), (-1, 4, 0, 5),
+     (8, 2, 1, 6), (1, 4, 0, 7), (-9, 2, -1, 6), (-2, 3, 0, 5), (-7, 1, -1, 6), (7, 2, 1, 6), (-6, 4, 0, 7),
+     (-2, 0, 0, 5), (9, 2, 1, 6), (-9, 3, -1, 6), (-6, 2, 0, 7), (7, 0, 1, 6), (-2, 1, 0, 5), (-7, 2, -1, 6),
+     (-6, 3, 0, 7), (7, 1, 1, 6), (-2, 2, 0, 5), (-7, 3, -1, 6), (9, 1, 0, 7), (9, 0, 1, 6), (-2, 4, 0, 5),
+     (-9, 4, -1, 6), (-6, 1, 0, 7), (6, 3, 1, 6), (2, 4, 1, 6), (-3, 2, 0, 5), (-7, 4, -1, 6), (-5, 3, 0, 7),
+     (6, 0, 1, 6), (-3, 3, 0, 5), (2, 0, 0, 7), (2, 2, 1, 6), (-3, 0, 0, 5), (2, 1, 0, 7), (2, 3, 1, 6),
+     (6, 1, 0, 5), (-5, 2, 0, 7), (6, 2, 1, 6), (-3, 1, 0, 5), (-5, 4, 0, 7), (-3, 4, 0, 5), (3, 3, 1, 6),
+     (-4, 1, 0, 7), (5, 3, 1, 6), (5, 2, 0, 5), (3, 0, 0, 7), (5, 0, 1, 6), (-4, 2, 0, 7), (-4, 3, 0, 5),
+     (3, 1, 0, 7), (5, 1, 1, 6), (4, 0, 0, 5), (3, 2, 0, 7), (4, 3, 1, 7), (4, 1, 1, 6), (-5, 1, 0, 5),
+     (-4, 4, 0, 7), (4, 2, 1, 6)),
+    ((-8, 4, -1, 7), (-7, 4, 0, 0), (-1, 1, 0, 6), (-1, 0, 0, 6), (-8, 3, -1, 7), (-7, 2, 0, 0), (-1, 2, 0, 6),
+     (-8, 2, -1, 7), (-7, 3, 0, 0), (8, 1, 1, 7), (-1, 3, 0, 6), (-7, 1, 0, 0), (8, 0, 1, 7), (-1, 4, 0, 6),
+     (8, 2, 1, 7), (-6, 3, 0, 0), (1, 4, 1, 7), (-2, 2, 0, 6), (1, 0, 0, 0), (7, 1, 1, 7), (-2, 3, 0, 6),
+     (1, 1, 0, 0), (7, 0, 1, 7), (-9, 2, -1, 7), (-6, 1, 0, 0), (-2, 0, 0, 6), (7, 2, 1, 7), (1, 2, 0, 0),
+     (-2, 1, 0, 6), (-9, 3, -1, 7), (1, 3, 1, 7), (-6, 2, 0, 0), (-2, 4, 0, 6), (-9, 4, -1, 7), (2, 3, 1, 7),
+     (-6, 4, 0, 0), (-3, 3, 0, 6), (6, 2, 1, 7), (-5, 1, 0, 0), (-3, 0, 0, 6), (9, 0, 1, 7), (2, 0, 0, 0),
+     (6, 3, 1, 7), (-5, 2, 0, 0), (9, 1, 1, 7), (-3, 4, 0, 6), (2, 1, 0, 0), (6, 0, 1, 7), (5, 3, 0, 6),
+     (9, 2, 1, 7), (-5, 3, 0, 0), (-4, 2, 0, 6), (6, 1, 1, 7), (2, 2, 0, 0), (2, 4, 1, 7), (-4, 3, 0, 6),
+     (-5, 4, 0, 0), (3, 1, 1, 7), (-4, 1, 0, 0), (4, 0, 0, 5), (5, 0, 1, 7), (5, 1, 0, 6), (-3, 1, 0, 0),
+     (3, 2, 1, 7), (5, 2, 0, 6), (3, 3, 1, 7), (-3, 2, 0, 0), (3, 0, 0, 5), (4, 3, 1, 7), (-4, 4, 0, 6),
+     (4, 2, 0, 6), (4, 1, 1, 7)),
 )
 
 
@@ -123,6 +156,7 @@
     return 1 + max([depth_of(y_next, d_next, part) for y_next, d_next, _ in receivers(y, d, part)], default=0)
 
 
+@functools.cache
 def sends_from(column):
     own = [(0, part, *entry) for part in range(len(PARTS)) for entry in receivers(column, 0, part)]
     own.sort(key=lambda entry: -depth_of(entry[2], entry[3], entry[1]))
@@ -130,6 +164,22 @@
         (d, part, *entry) for d, part, _, _ in ROUTES[column] for entry in receivers(column, d, part)
     ]
     return own + relayed
+
+
+def turn_of(column, slot, part):
+    return max([0] + [turn for turn, entry in enumerate(ROUTES[column]) if entry[:2] == (slot, part)])
+
+
+def sent_before(column, first, last):
+    return [
+        number
+        for number, entry in enumerate(sends_from(column))
+        if first <= turn_of(column, entry[0], entry[1]) < last
+    ]
+
+
+def even_turns(column):
+    return 1 + max(turn for turn, entry in enumerate(ROUTES[column]) if entry[0] % 2 == 0)
 
 
 MOST_SENDS = max(len(sends_from(column)) for column in range(LINE))
@@ -238,17 +288,34 @@
 
     window = pl.ds(MARGIN * LANES, WIDTH)
 
+    def keep_squares(product, odd):
+        for order, slot in enumerate(range(odd, SLOTS, 2)):
+            kept = pat_ref[0, slot].astype(jnp.float32)
+            part = product[order * BLOCK:(order + 1) * BLOCK, :] * kept
+            squares[(1 + slot) * BLOCK:(2 + slot) * BLOCK, :] = part
+            low[(1 + slot) * BLOCK:(2 + slot) * BLOCK, :] = part.astype(jnp.bfloat16)
+
+    def drain(step, column, number):
+        entry = sends_from(column)[number]
+
+        @pl.when(sent_when(column, entry[0], entry[4]))
+        def _():
+            copy(step, number, *entry).wait_send()
+
     def purify(step, _):
         def offer(column):
             for number, entry in enumerate(sends_from(column)):
                 if entry[0] == 0:
-                    @pl.when(sent_when(column, 0, entry[4]))
+                    @pl.when(sent_when(column, entry[0], entry[4]))
                     def _():
                         copy(step, number, *entry).start()
 
-        def relay(column):
+        def relay(column, first, last):
             sends = sends_from(column)
-            for d, part, _, _ in ROUTES[column]:
+            for turn, (d, part, _, _) in enumerate(ROUTES[column]):
+                if not first <= turn < last:
+                    continue
+
                 @pl.when(there[line_of(column, d)])
                 def _():
                     arrival(step, column, d, part).wait_recv()
@@ -259,6 +326,15 @@
                         def _():
                             copy(step, number, *entry).start()
 
+                for number in sent_before(column, turn - DELAY, turn - DELAY + 1):
+                    drain(step, column, number)
+
+        def relay_even(column):
+            relay(column, 0, even_turns(column))
+
+        def relay_odd(column):
+            relay(column, even_turns(column), len(ROUTES[column]))
+
         each_column(offer)
 
         @pl.when(step == 0)
@@ -273,20 +349,16 @@
                 part = squares[2 * tile * BLOCK:(2 + 2 * tile) * BLOCK, :]
                 shifted[:, tile * LANES:(1 + tile) * LANES] = part.T.astype(jnp.bfloat16)
 
-        each_column(relay)
+        each_column(relay_even)
         own = band[rows_of(step, 0), window]
         even_rows = band[pl.ds(pl.multiple_of(step * FULL, BLOCK), EVENS), window]
-        odd_rows = band[pl.ds(pl.multiple_of(step * FULL + EVENS, BLOCK), ODDS), window]
         across = (((1,), (1,)), ((), ()))
         even_square = lax.dot_general(even_rows, own, across, preferred_element_type=jnp.float32)
+        keep_squares(even_square, 1)
+        each_column(relay_odd)
+        odd_rows = band[pl.ds(pl.multiple_of(step * FULL + EVENS, BLOCK), ODDS), window]
         odd_square = lax.dot_general(odd_rows, shifted[...], across, preferred_element_type=jnp.float32)
-        for slot in range(SLOTS):
-            order = (slot - 1) // 2 if slot % 2 else slot // 2
-            source = even_square if slot % 2 else odd_square
-            kept = pat_ref[0, slot].astype(jnp.float32)
-            part = source[order * BLOCK:(order + 1) * BLOCK, :] * kept
-            squares[(1 + slot) * BLOCK:(2 + slot) * BLOCK, :] = part
-            low[(1 + slot) * BLOCK:(2 + slot) * BLOCK, :] = part.astype(jnp.bfloat16)
+        keep_squares(odd_square, 0)
         even_cube = jnp.dot(even_rows, low[BLOCK:BLOCK + WIDTH, :], preferred_element_type=jnp.float32)
         odd_cube = jnp.dot(odd_rows, low[0:WIDTH, :], preferred_element_type=jnp.float32)
         for slot in range(SLOTS):
@@ -315,13 +387,12 @@
         out_ref[:, tile * LANES:tile * LANES + wide] = part[:, :wide]
 
     def finish(step, _):
-        def drain(column):
-            for number, entry in enumerate(sends_from(column)):
-                @pl.when(sent_when(column, entry[0], entry[4]))
-                def _():
-                    copy(step, number, *entry).wait_send()
-
-        each_column(drain)
+        def rest(column):
+            turns = len(ROUTES[column])
+            for number in sent_before(column, turns - DELAY, turns):
+                drain(step, column, number)
+
+        each_column(rest)
         return 0
 
     lax.fori_loop(0, STEPS, finish, 0)

time: 62.7 us -> 61.4 us (0.979)
  Pallas kernels: 60.2 us -> 58.9 us
    pallas_call x1, Pallas kernels: 60.2 us -> 58.9 us  [local(): pl.pallas_call(functools.partial(kernel, lines, columns), out_shape=jax.S...]
where the time goes in v4:
time: 61.4 us; the launch traced here: 61.3 us
  Pallas kernels  58.9 us (96%)
  local copies, waits for them, and re-layouts  2.35 us (4%)
    pallas_call x1, Pallas kernels, local(): pl.pallas_call(functools.partial(kernel, lines, columns), out_shape=jax.S...  58.9 us
    unnamed x5, local copies, waits for them, and re-layouts  2.35 us

profile of v4, /device:TPU:1, one launch (start us, length us, event | category | flops | bytes accessed | tf_op | source)
XLA Modules:
  0.0 61.3 jit_solution(11285892317797353431)
XLA Ops:
  0.0 0.0 copy-start
  0.0 1.0 %copy-done = f32[64,1216]{1,0:T(8,128)S(1)} copy-done((f32[64,1216]{1,0:T(8,128)S(1)}, f32[64,1216]{1,0:T(8,128)}, u32[]{:S(2)}) %copy-start) | copy-done | bytes 311320
  1.0 0.0 copy-start.1
  1.0 0.7 %copy-done.1 = s32[1,19]{1,0:T(1,128)S(1)} copy-done((s32[1,19]{1,0:T(1,128)S(1)}, s32[1,19]{1,0:T(1,128)}, u32[]{:S(2)}) %copy-start.1) | copy-done | bytes 100
  1.6 58.9 %shard_map.28 = f32[64,1216]{1,0:T(8,128)S(1)} custom-call(f32[64,1216]{1,0:T(8,128)S(1)} %copy-done, s32[1,19]{1,0:T(1,128)S(1)} %copy-done.1), custom_call_target="tpu_custom_call" | custom-call | tf_op jit(solution)/shard_map/pallas_call | solution.py:406
  60.6 0.7 %copy.4 = f32[64,1216]{1,0:T(8,128)} copy(f32[64,1216]{1,0:T(8,128)S(1)} %shard_map.28) | data formatting | bytes 622592
Async XLA Ops:
  0.0 1.0 %copy-start = (f32[64,1216]{1,0:T(8,128)S(1)}, f32[64,1216]{1,0:T(8,128)}, u32[]{:S(2)}) copy-start(f32[64,1216]{1,0:T(8,128)} %dens_hbm.1) | copy-start | bytes 933892
  1.0 0.7 %copy-start.1 = (s32[1,19]{1,0:T(1,128)S(1)}, s32[1,19]{1,0:T(1,128)}, u32[]{:S(2)}) copy-start(s32[1,19]{1,0:T(1,128)} %pat_hbm.1) | copy-start | bytes 232

commit v5 on v4

--- a/solution.py
+++ b/solution.py
@@ -190,11 +190,7 @@
     return sorted(found | {(line, y) for _, _, y, _, line in sends_from(column)})
 
 
-def kernel(lines, columns, dens_hbm, pat_hbm, out_ref, dens_ref, pat_ref, band, shifted, squares, low, load_sem, send_sem, recv_sem):
-    load = pltpu.make_async_copy(dens_hbm, dens_ref, load_sem.at[0])
-    load.start()
-    load_pattern = pltpu.make_async_copy(pat_hbm, pat_ref, load_sem.at[1])
-    load_pattern.start()
+def kernel(lines, columns, dens_ref, pat_ref, out_ref, band, shifted, squares, low, send_sem, recv_sem):
     me = lax.axis_index("row") * columns + lax.axis_index("col")
     my_line = me // LINE
     my_column = lax.rem(me, LINE)
@@ -257,11 +253,9 @@
         pl.semaphore_wait(barrier, count)
 
     each_column(greet)
-    load.wait()
     padded = jnp.concatenate([dens_ref[...], jnp.zeros((BLOCK, WIDTH - FULL), jnp.float32)], axis=1)
     band[rows_of(0, 0), MARGIN * LANES:(MARGIN + TILES) * LANES] = padded.astype(jnp.bfloat16)
     each_column(meet)
-    load_pattern.wait()
 
     def clear():
         for step in range(STEPS):
@@ -407,18 +401,15 @@
             functools.partial(kernel, lines, columns),
             out_shape=jax.ShapeDtypeStruct((BLOCK, FULL), jnp.float32),
             in_specs=[
-                pl.BlockSpec(memory_space=pltpu.HBM),
-                pl.BlockSpec(memory_space=pltpu.HBM),
+                pl.BlockSpec(memory_space=pltpu.VMEM),
+                pl.BlockSpec(memory_space=pltpu.SMEM),
             ],
             out_specs=pl.BlockSpec(memory_space=pltpu.VMEM),
             scratch_shapes=[
-                pltpu.VMEM((BLOCK, FULL), jnp.float32),
-                pltpu.SMEM((1, SLOTS), jnp.int32),
                 pltpu.VMEM((STEPS * FULL, STORED * LANES), jnp.bfloat16),
                 pltpu.VMEM((BLOCK, WIDTH), jnp.bfloat16),
                 pltpu.VMEM(((SLOTS + 2) * BLOCK, BLOCK), jnp.float32),
                 pltpu.VMEM(((SLOTS + 2) * BLOCK, BLOCK), jnp.bfloat16),
-                pltpu.SemaphoreType.DMA((2,)),
                 pltpu.SemaphoreType.DMA((STEPS, MOST_SENDS)),
                 pltpu.SemaphoreType.DMA((STEPS, len(PARTS) * SLOTS)),
             ],

time: 61.4 us -> 61.6 us (level)
  no operation moved by 1% of the time
where the time goes in v5:
time: 61.6 us; the launch traced here: 61.5 us
  Pallas kernels  59.1 us (96%)
  local copies, waits for them, and re-layouts  2.35 us (4%)
    pallas_call x1, Pallas kernels, local(): pl.pallas_call(functools.partial(kernel, lines, columns), out_shape=jax.S...  59.1 us
    unnamed x5, local copies, waits for them, and re-layouts  2.35 us

profile of v5, /device:TPU:1, one launch (start us, length us, event | category | flops | bytes accessed | tf_op | source)
XLA Modules:
  0.0 61.5 jit_solution(16938761426588512388)
XLA Ops:
  0.0 0.0 copy-start
  0.0 1.0 %copy-done = f32[64,1216]{1,0:T(8,128)S(1)} copy-done((f32[64,1216]{1,0:T(8,128)S(1)}, f32[64,1216]{1,0:T(8,128)}, u32[]{:S(2)}) %copy-start) | copy-done | bytes 311320
  1.0 0.0 copy-start.1
  1.0 0.7 %copy-done.1 = s32[1,19]{1,0:T(1,128)S(1)} copy-done((s32[1,19]{1,0:T(1,128)S(1)}, s32[1,19]{1,0:T(1,128)}, u32[]{:S(2)}) %copy-start.1) | copy-done | bytes 100
  1.6 59.1 %shard_map.28 = f32[64,1216]{1,0:T(8,128)S(1)} custom-call(f32[64,1216]{1,0:T(8,128)S(1)} %copy-done, s32[1,19]{1,0:T(1,128)S(1)} %copy-done.1), custom_call_target="tpu_custom_call" | custom-call | tf_op jit(solution)/shard_map/pallas_call | solution.py:400
  60.8 0.7 %copy.4 = f32[64,1216]{1,0:T(8,128)} copy(f32[64,1216]{1,0:T(8,128)S(1)} %shard_map.28) | data formatting | bytes 622592
Async XLA Ops:
  0.0 1.0 %copy-start = (f32[64,1216]{1,0:T(8,128)S(1)}, f32[64,1216]{1,0:T(8,128)}, u32[]{:S(2)}) copy-start(f32[64,1216]{1,0:T(8,128)} %dens_ref.1) | copy-start | bytes 933892
  1.0 0.7 %copy-start.1 = (s32[1,19]{1,0:T(1,128)S(1)}, s32[1,19]{1,0:T(1,128)}, u32[]{:S(2)}) copy-start(s32[1,19]{1,0:T(1,128)} %pat_ref.1) | copy-start | bytes 232
